TPU v7x, 32 devices: a whole 2x2x4 slice. The times are simulated.
32 devices in a mesh: pairs: 2 (over y), ctx: 8 (over z, x), head: 2 (over core).
Axes of the slice: x: 2, y: 2, z: 4, core: 2. Of those that a mesh axis runs over, the one named last changes fastest.
Arguments:
- hidden: bfloat16 [16, 2, 8192], P(('pairs', 'ctx')), parts along dimension 0, may hold values from -6 to 6
- wq: bfloat16 [8192, 4096], P('ctx', 'head'), may hold values from -0.0625 to 0.0625
- wkv: bfloat16 [2, 8192, 512], P(None, 'ctx', 'head'), may hold values from -0.0625 to 0.0625
- bias_q: bfloat16 [4096], P('head'), may hold values from -5.2 to 5.2
- bias_kv: bfloat16 [2, 512], P(None, 'head'), may hold values from -5.2 to 5.2
- key_value_cache: bfloat16 [2, 8192, 512], P(None, ('pairs', 'ctx'), 'head'), parts along dimension 1, may hold values from -46 to 46, as said below
- prompt_len: int32 [2], P('pairs'), parts along dimension 0, may hold values from 512 to 4096
- resp_len: int32 [4], P('pairs'), parts along dimension 0, may hold values from 2 to 8
Outputs:
- attn_out: bfloat16 [16, 2, 4096], P(('pairs', 'ctx'), None, 'head'), parts along dimension 0
There are 2 independent parts, one for each index of `pairs`. A program takes and returns all parts, laid end to end along the dimension named above; an argument that names none is the same for every part. Nothing has to cross between parts.
Inputs may be any that keep to these rules, and one draw needn't show every extreme that they name: `key_value_cache`: entries beyond prompt_len are padding and must not be attended to. Prompt positions from prompt_len on are padding. Token slots of response r from resp_len[r] on are padding.
All inputs are finite; a program needn't handle non-finite values.
Results may differ from a plain program's by a relative error of at most 0.025.
Values may be sent and summed in bfloat16 or wider, within the bound.
No kernel may reach another device: no remote copies, remote signals or barrier semaphores. Data moves between devices by JAX's collectives and lax.ppermute only.
A program may use at most 64 MiB of HBM per device.

v0:
```python
import jax
import jax.numpy as jnp
from jax import lax
from jax.sharding import PartitionSpec as P

HEAD_SIZE = 128


NEG_FILL = -1e30


def shards(hidden, wq, wkv, bias_q, bias_kv, key_value_cache, prompt_len, resp_len):
    tok_dev = hidden.shape[0]
    ctx_index = lax.axis_index("ctx")
    resp_tokens = tok_dev * lax.axis_size("ctx")
    q_width = wq.shape[1]
    k_width = wkv.shape[2]
    kv_local = k_width // HEAD_SIZE
    query_group_width = q_width // k_width
    score_scale = HEAD_SIZE ** (-0.5)
    row_count = 2 * tok_dev
    columns = lax.all_to_all(hidden, "ctx", split_axis=2, concat_axis=0, tiled=True)
    flat_rows = columns.reshape(2 * resp_tokens, columns.shape[2])
    weights_all = jnp.concatenate((wq, wkv[0], wkv[1]), axis=1)
    bias_all = jnp.concatenate((bias_q, bias_kv[0], bias_kv[1])).astype(jnp.float32)
    summed = lax.psum(jnp.dot(flat_rows, weights_all, preferred_element_type=jnp.float32), "ctx")
    projected = (summed + bias_all).astype(jnp.bfloat16)
    owned = lax.dynamic_slice_in_dim(projected, ctx_index * row_count, row_count, 0)
    query_rows = projected[:, :q_width].reshape(
        2 * resp_tokens, kv_local, query_group_width, HEAD_SIZE
    )
    cache_len = key_value_cache.shape[1]
    key_block = min(512, cache_len)
    block_count = cache_len // key_block
    prompt_key_rows = key_value_cache[0].reshape(block_count, key_block, kv_local, HEAD_SIZE)
    prompt_value_rows = key_value_cache[1].reshape(block_count, key_block, kv_local, HEAD_SIZE)
    first_slot = ctx_index * cache_len
    live_limit = prompt_len[0]

    def visit(carry, inputs):
        running_max, running_sum, weighted = carry
        block_keys, block_values, block_index = inputs
        scores = (
            jnp.einsum("rgjd,kgd->grjk", query_rows, block_keys, preferred_element_type=jnp.float32)
            * score_scale
        )
        position = first_slot + block_index * key_block + lax.iota(jnp.int32, key_block)
        is_live = position < live_limit
        scores = jnp.where(is_live, scores, NEG_FILL)
        new_max = jnp.maximum(running_max, jnp.max(scores, axis=-1))
        unscaled = jnp.where(is_live, jnp.exp(scores - new_max[..., None]), 0.0)
        factor = jnp.exp(running_max - new_max)
        running_sum = running_sum * factor + jnp.sum(unscaled, axis=-1)
        weighted = weighted * factor[..., None] + jnp.einsum(
            "grjk,kgd->grjd",
            unscaled.astype(jnp.bfloat16),
            block_values,
            preferred_element_type=jnp.float32,
        )
        return ((new_max, running_sum, weighted), None)

    statistic_shape = (kv_local, 2 * resp_tokens, query_group_width)
    start_state = (
        jnp.full(statistic_shape, NEG_FILL, jnp.float32),
        jnp.zeros(statistic_shape, jnp.float32),
        jnp.zeros(statistic_shape + (HEAD_SIZE,), jnp.float32),
    )
    closing_state, unused = lax.scan(
        visit,
        start_state,
        (prompt_key_rows, prompt_value_rows, jnp.arange(block_count, dtype=jnp.int32)),
    )
    owned_q = owned[:, :q_width].reshape(tok_dev, 2, kv_local, query_group_width, HEAD_SIZE)
    fresh_key_rows = projected[:, q_width : q_width + k_width].reshape(
        resp_tokens, 2, kv_local, HEAD_SIZE
    )
    fresh_value_rows = projected[:, q_width + k_width :].reshape(
        resp_tokens, 2, kv_local, HEAD_SIZE
    )
    self_scores = (
        jnp.einsum("trgjd,urgd->gtrju", owned_q, fresh_key_rows, preferred_element_type=jnp.float32)
        * score_scale
    )
    token_pos = ctx_index * tok_dev + lax.iota(jnp.int32, tok_dev)
    key_pos = lax.iota(jnp.int32, resp_tokens)
    self_live = (key_pos[None, None, :] <= token_pos[:, None, None]) & (
        key_pos[None, None, :] < resp_len[None, :, None]
    )
    self_live = self_live[None, :, :, None, :]
    self_scores = jnp.where(self_live, self_scores, NEG_FILL)
    self_max = jnp.max(self_scores, axis=-1)
    self_weights = jnp.where(self_live, jnp.exp(self_scores - self_max[..., None]), 0.0)
    self_sum = jnp.sum(self_weights, axis=-1)
    self_acc = jnp.einsum(
        "gtrju,urgd->gtrjd",
        self_weights.astype(jnp.bfloat16),
        fresh_value_rows,
        preferred_element_type=jnp.float32,
    )
    lead_shape = (1, kv_local, resp_tokens, 2, query_group_width)
    remote_max, remote_sum, remote_acc = (
        lax.all_to_all(
            closing_state[0].reshape(lead_shape), "ctx", split_axis=2, concat_axis=0, tiled=True
        ),
        lax.all_to_all(
            closing_state[1].reshape(lead_shape), "ctx", split_axis=2, concat_axis=0, tiled=True
        ),
        lax.all_to_all(
            closing_state[2].reshape(lead_shape + (HEAD_SIZE,)),
            "ctx",
            split_axis=2,
            concat_axis=0,
            tiled=True,
        ),
    )
    overall = jnp.maximum(jnp.max(remote_max, axis=0), self_max)
    remote_factor = jnp.exp(remote_max - overall[None])
    prompt_acc = jnp.sum(remote_factor[..., None] * remote_acc, axis=0)
    prompt_total = jnp.sum(remote_factor * remote_sum, axis=0)
    self_factor = jnp.exp(self_max - overall)
    numerator = prompt_acc + self_factor[..., None] * self_acc
    denominator = prompt_total + self_factor * self_sum
    result = numerator / denominator[..., None]
    row_live = token_pos[:, None] < resp_len[None, :]
    result = jnp.where(row_live[None, :, :, None, None], result, 0.0)
    return jnp.transpose(result, (1, 2, 0, 3, 4)).reshape(tok_dev, 2, q_width).astype(jnp.bfloat16)


def solution(mesh):
    return jax.shard_map(
        shards,
        mesh=mesh,
        in_specs=(
            P(("pairs", "ctx"), None, None),
            P("ctx", "head"),
            P(None, "ctx", "head"),
            P("head"),
            P(None, "head"),
            P(None, ("pairs", "ctx"), "head"),
            P("pairs"),
            P("pairs"),
        ),
        out_specs=P(("pairs", "ctx"), None, "head"),
        check_vma=False,
    )
```

profile of v0, /device:TPU:0, one launch (start us, length us, event | category | flops | bytes accessed | tf_op | source)
XLA Modules:
  0.0 205.0 jit_solution(12979786244044143791)
XLA Ops:
  6.5 8.2 %copy.38 = bf16[1,2,8192]{1,0,2:T(2,128)(2,1)} copy(bf16[1,2,8192]{2,1,0:T(2,128)(2,1)} %param.8) | data formatting | bytes 65536 | tf_op args[0]
  14.8 0.5 broadcast.132
  15.3 0.0 copy-start
  15.3 45.3 %reduce.10 = bf16[8192,2]{1,0:T(8,128)(2,1)S(1)} reduce(bf16[8192,1,2]{2,1,0:T(2,128)(2,1)} %bitcast.123, bf16[]{:T(256)} %broadcast.132), dimensions={1}, to_apply=%bitcast.111.reduce_sub_computation | reduce | bytes 65538
  60.6 0.0 copy-start.3
  60.6 0.0 copy-start.2
  60.6 3.8 %reshape.289 = bf16[8,2,1024]{2,1,0:T(2,128)(2,1)} reshape(bf16[8192,2]{1,0:T(8,128)(2,1)S(1)} %reduce.10) | data formatting | bytes 65536
  64.4 7.3 %all-to-all-start = ((bf16[8,2,1024]{2,1,0:T(2,128)(2,1)}), bf16[8,2,1024]{2,1,0:T(2,128)(2,1)S(1)}, u32[]{:S(2)}, u32[]{:S(2)}) async-start(bf16[8,2,1024]{2,1,0:T(2,128)(2,1)} %reshape.289), calls=%async_computation | async-start | bytes 65536 | tf_op jit(solution)/shard_map/all_to_all | solution.py:22
  71.7 0.0 all-reduce.2.cloned.1.call-start
  71.8 1.1 fusion.45
  72.8 0.0 copy-done
  72.8 0.1 slice_bitcast_fusion.1
  73.6 0.0 copy-done.3
  73.6 0.1 compare_and_fusion
  73.7 0.0 copy-done.2
  73.7 4.7 %all-to-all-done = bf16[8,2,1024]{2,1,0:T(2,128)(2,1)S(1)} async-done(((bf16[8,2,1024]{2,1,0:T(2,128)(2,1)}), bf16[8,2,1024]{2,1,0:T(2,128)(2,1)S(1)}, u32[]{:S(2)}, u32[]{:S(2)}) %all-to-all-start) | async-done | bytes 32800 | tf_op jit(solution)/shard_map/all_to_all | solution.py:22
  78.4 6.3 %reshape.290 = bf16[8192,1,2]{2,1,0:T(2,128)(2,1)} reshape(bf16[8,2,1024]{2,1,0:T(2,128)(2,1)S(1)} %all-to-all-done) | data formatting | bytes 65536
  84.7 8.1 %copy.39 = bf16[1,2,8192]{2,1,0:T(2,128)(2,1)S(1)} copy(bf16[1,2,8192]{1,0,2:T(2,128)(2,1)} %bitcast.124) | data formatting | bytes 65536 | tf_op jit(solution)/shard_map/all_to_all | solution.py:22
  92.8 0.0 copy-start.1
  92.9 3.3 %fusion.6 = f32[16,2560]{1,0:T(8,128)} fusion(bf16[16,1024]{1,0:T(8,128)(2,1)S(1)} %reshape.278, bf16[1024,256]{1,0:T(8,128)(2,1)S(1)} %get-tuple-element.26, bf16[1024,256]{1,0:T(8,128)(2,1)S(1)} %get-tuple-element.25, bf16[1024,2048]{1,0:T(8,128)(2,1)} %param.9), kind=kOutput, calls=%fused_computation.6 | convolution fusion | flops 99614720 | bytes 5439488 | tf_op jit(solution)/shard_map/dot_general | solution.py:26
  96.2 0.0 all-reduce.2.cloned.1.call-update
  96.2 0.1 copy.62
  96.4 0.1 copy.61
  96.5 0.0 copy-done.1
  96.6 67.2 %all-reduce.2.cloned.1.call-done = f32[16,2560]{1,0:T(8,128)} async-done(((f32[16,2560]{1,0:T(8,128)}), f32[16,2560]{1,0:T(8,128)}) %all-reduce.2.cloned.1.call-update) | async-done | bytes 163856 | tf_op jit(solution)/shard_map/psum | solution.py:26
  163.8 0.9 add_convert_fusion
  164.7 0.3 fusion.47
  165.1 0.6 copy.44
  165.7 4.4 %all-to-all-start.1 = ((f32[1,2,8,2,8]{4,3,1,0,2:T(2,128)}), f32[1,2,8,2,8]{4,3,1,0,2:T(2,128)S(1)}, u32[]{:S(2)}, u32[]{:S(2)}) async-start(f32[1,2,8,2,8]{4,3,1,0,2:T(2,128)} %copy.44), calls=%async_computation.1 | async-start | bytes 32768 | tf_op jit(solution)/shard_map/all_to_all | solution.py:102
  170.1 0.2 fusion.18
  170.4 0.3 convolution_add_fusion
  170.6 0.1 fusion.48
  170.8 0.1 fusion.29
  170.9 0.6 copy.49
  171.5 0.6 copy.52
  172.1 4.5 %all-to-all-done.1 = f32[1,2,8,2,8]{4,3,1,0,2:T(2,128)S(1)} async-done(((f32[1,2,8,2,8]{4,3,1,0,2:T(2,128)}), f32[1,2,8,2,8]{4,3,1,0,2:T(2,128)S(1)}, u32[]{:S(2)}, u32[]{:S(2)}) %all-to-all-start.1) | async-done | bytes 1056 | tf_op jit(solution)/shard_map/all_to_all | solution.py:102
  176.6 3.3 %all-to-all-start.3 = ((f32[1,2,8,2,8]{4,3,1,0,2:T(2,128)}), f32[1,2,8,2,8]{4,3,1,0,2:T(2,128)S(1)}, u32[]{:S(2)}, u32[]{:S(2)}) async-start(f32[1,2,8,2,8]{4,3,1,0,2:T(2,128)} %copy.52), calls=%async_computation.3 | async-start | bytes 32768 | tf_op jit(solution)/shard_map/all_to_all | solution.py:105
  180.0 6.5 %all-to-all-done.3 = f32[1,2,8,2,8]{4,3,1,0,2:T(2,128)S(1)} async-done(((f32[1,2,8,2,8]{4,3,1,0,2:T(2,128)}), f32[1,2,8,2,8]{4,3,1,0,2:T(2,128)S(1)}, u32[]{:S(2)}, u32[]{:S(2)}) %all-to-all-start.3) | async-done | bytes 1056 | tf_op jit(solution)/shard_map/all_to_all | solution.py:105
  186.5 3.4 %all-to-all-start.2 = ((f32[1,2,8,2,8,128]{5,4,3,1,0,2:T(8,128)}), f32[1,2,8,2,8,128]{5,4,3,1,0,2:T(8,128)S(1)}, u32[]{:S(2)}, u32[]{:S(2)}) async-start(f32[1,2,8,2,8,128]{5,4,3,1,0,2:T(8,128)} %copy.49), calls=%async_computation.2 | async-start | bytes 262144 | tf_op jit(solution)/shard_map/all_to_all | solution.py:108
  190.0 7.2 %all-to-all-done.2 = f32[1,2,8,2,8,128]{5,4,3,1,0,2:T(8,128)S(1)} async-done(((f32[1,2,8,2,8,128]{5,4,3,1,0,2:T(8,128)}), f32[1,2,8,2,8,128]{5,4,3,1,0,2:T(8,128)S(1)}, u32[]{:S(2)}, u32[]{:S(2)}) %all-to-all-start.2) | async-done | bytes 131104 | tf_op jit(solution)/shard_map/all_to_all | solution.py:108
  197.2 0.1 fusion.24
  197.3 0.2 fusion.15
  197.5 0.6 convert_element_type.36
  (22 shorter events, 0.3 us)
Async XLA Ops:
  15.3 57.6 %copy-start = (bf16[2,1024,256]{2,1,0:T(8,128)(2,1)S(1)}, bf16[2,1024,256]{2,1,0:T(8,128)(2,1)}, u32[]{:S(2)}) copy-start(bf16[2,1024,256]{2,1,0:T(8,128)(2,1)} %param.10) | copy-start | bytes 3145732
  60.6 13.0 %copy-start.3 = (s32[2]{0:T(128)S(1)}, s32[2]{0:T(128)}, u32[]{:S(2)}) copy-start(s32[2]{0:T(128)} %param.15) | copy-start | bytes 28
  60.6 13.1 %copy-start.2 = (bf16[2,256]{1,0:T(2,128)(2,1)S(1)}, bf16[2,256]{1,0:T(2,128)(2,1)}, u32[]{:S(2)}) copy-start(bf16[2,256]{1,0:T(2,128)(2,1)} %param.12) | copy-start | bytes 3076
  64.4 14.0 %all-to-all-start = ((bf16[8,2,1024]{2,1,0:T(2,128)(2,1)}), bf16[8,2,1024]{2,1,0:T(2,128)(2,1)S(1)}, u32[]{:S(2)}, u32[]{:S(2)}) async-start(bf16[8,2,1024]{2,1,0:T(2,128)(2,1)} %reshape.289), calls=%async_computation | async-start | bytes 65536 | tf_op jit(solution)/shard_map/all_to_all | solution.py:22
  71.7 92.0 %all-reduce.2.cloned.1.call-start = ((), (), s32[]{:S(2)}) async-start(), calls=%async_computation.4 | async-start | bytes 327680 | tf_op jit(solution)/shard_map/psum | solution.py:26
  92.8 3.7 %copy-start.1 = (bf16[2048]{0:T(1024)(128)(2,1)S(1)}, bf16[2048]{0:T(1024)(128)(2,1)}, u32[]{:S(2)}) copy-start(bf16[2048]{0:T(1024)(128)(2,1)} %param.11) | copy-start | bytes 12292
  165.7 11.0 %all-to-all-start.1 = ((f32[1,2,8,2,8]{4,3,1,0,2:T(2,128)}), f32[1,2,8,2,8]{4,3,1,0,2:T(2,128)S(1)}, u32[]{:S(2)}, u32[]{:S(2)}) async-start(f32[1,2,8,2,8]{4,3,1,0,2:T(2,128)} %copy.44), calls=%async_computation.1 | async-start | bytes 32768 | tf_op jit(solution)/shard_map/all_to_all | solution.py:102
  176.6 9.9 %all-to-all-start.3 = ((f32[1,2,8,2,8]{4,3,1,0,2:T(2,128)}), f32[1,2,8,2,8]{4,3,1,0,2:T(2,128)S(1)}, u32[]{:S(2)}, u32[]{:S(2)}) async-start(f32[1,2,8,2,8]{4,3,1,0,2:T(2,128)} %copy.52), calls=%async_computation.3 | async-start | bytes 32768 | tf_op jit(solution)/shard_map/all_to_all | solution.py:105
  186.5 10.7 %all-to-all-start.2 = ((f32[1,2,8,2,8,128]{5,4,3,1,0,2:T(8,128)}), f32[1,2,8,2,8,128]{5,4,3,1,0,2:T(8,128)S(1)}, u32[]{:S(2)}, u32[]{:S(2)}) async-start(f32[1,2,8,2,8,128]{5,4,3,1,0,2:T(8,128)} %copy.49), calls=%async_computation.2 | async-start | bytes 262144 | tf_op jit(solution)/shard_map/all_to_all | solution.py:108
Sparse Core Ops, SparseCore 0:
  96.3 67.3 all-reduce.1
where the time goes:
time: 206 us; the launch traced here: 205 us
  waiting for transfers between devices  90.1 us (44%)
  other arithmetic  46.9 us (23%)
  local copies, waits for them, and re-layouts  31 us (15%)
  starting transfers between devices  18.4 us (9%)
  between operations  14.3 us (7%)
  matrix products  4.29 us (2%)
    psum x1, waiting for transfers between devices, shards(): lax.psum(jnp.dot(flat_rows, weights_all, preferred_element_type=jnp.float...  67.2 us
    unnamed x1, other arithmetic  45.3 us
    unnamed x18, local copies, waits for them, and re-layouts  19.2 us
    all_to_all x2, local copies, waits for them, and re-layouts, shards(): lax.all_to_all(hidden, 'ctx', split_axis=2, concat_axis=0, tiled=True)  8.11 us
    all_to_all x1, starting transfers between devices, shards(): lax.all_to_all(hidden, 'ctx', split_axis=2, concat_axis=0, tiled=True)  7.28 us
    all_to_all x1, waiting for transfers between devices, shards(): lax.all_to_all(closing_state[2].reshape(lead_shape + (HEAD_SIZE,)), 'ctx'...  7.2 us
    all_to_all x1, waiting for transfers between devices, shards(): lax.all_to_all(closing_state[1].reshape(lead_shape), 'ctx', split_axis=2,...  6.48 us
    all_to_all x1, waiting for transfers between devices, shards(): lax.all_to_all(hidden, 'ctx', split_axis=2, concat_axis=0, tiled=True)  4.69 us
  transfers between devices with their start and end apart: 5, of which 5 were waited for; matrix products, arithmetic and copies ran while one was open for 2% of the time, Pallas kernels for 0%

commit v1 on v0

v1 whole, which is shorter than its diff:
```python
import jax
import jax.numpy as jnp
from jax import lax
from jax.sharding import PartitionSpec as P

HEAD_SIZE = 128
NEG_FILL = -1e30


def split_columns(rows, parts):
    width = rows.shape[1] // parts
    if parts <= 16:
        return jnp.stack([rows[:, d * width : (d + 1) * width] for d in range(parts)])
    return jnp.swapaxes(rows.reshape(rows.shape[0], parts, width), 0, 1)


def sum_over(value, axis, size):
    bit = 1
    while bit < size:
        pairs = [(d, d ^ bit) for d in range(size)]
        other = lax.ppermute(value.astype(jnp.bfloat16), axis, pairs)
        value = value + other.astype(jnp.float32)
        bit *= 2
    return value


def shards(hidden, wq, wkv, bias_q, bias_kv, key_value_cache, prompt_len, resp_len):
    tok_dev = hidden.shape[0]
    size = lax.axis_size("ctx")
    ctx_index = lax.axis_index("ctx")
    resp_tokens = tok_dev * size
    q_width = wq.shape[1]
    k_width = wkv.shape[2]
    kv_local = k_width // HEAD_SIZE
    group = q_width // k_width
    scale = HEAD_SIZE ** (-0.5)
    row_count = 2 * tok_dev
    rows = 2 * resp_tokens

    sent = split_columns(hidden.reshape(row_count, hidden.shape[2]), size)
    columns = lax.all_to_all(sent, "ctx", split_axis=0, concat_axis=0, tiled=True)
    flat_rows = columns.reshape(rows, columns.shape[2])
    partial = jnp.concatenate(
        (
            jnp.dot(flat_rows, wq, preferred_element_type=jnp.float32),
            jnp.dot(flat_rows, wkv[0], preferred_element_type=jnp.float32),
            jnp.dot(flat_rows, wkv[1], preferred_element_type=jnp.float32),
        ),
        axis=1,
    )
    bias_all = jnp.concatenate((bias_q, bias_kv[0], bias_kv[1])).astype(jnp.float32)
    projected = (sum_over(partial, "ctx", size) + bias_all).astype(jnp.bfloat16)
    query = projected[:, :q_width].reshape(rows, kv_local, group, HEAD_SIZE)

    cache_len = key_value_cache.shape[1]
    keys = key_value_cache[0].reshape(cache_len, kv_local, HEAD_SIZE)
    values = key_value_cache[1].reshape(cache_len, kv_local, HEAD_SIZE)
    live = ctx_index * cache_len + lax.iota(jnp.int32, cache_len) < prompt_len[0]
    scores = jnp.einsum("rgjd,kgd->rgjk", query, keys, preferred_element_type=jnp.float32) * scale
    scores = jnp.where(live, scores, NEG_FILL)
    peak = jnp.max(scores, axis=-1)
    weights = jnp.where(live, jnp.exp(scores - peak[..., None]), 0.0)
    total = jnp.sum(weights, axis=-1)
    acc = jnp.einsum(
        "rgjk,kgd->rgjd", weights.astype(jnp.bfloat16), values, preferred_element_type=jnp.float32
    )
    any_live = total > 0.0
    safe = jnp.where(any_live, total, 1.0)
    lse = jnp.where(any_live, peak + jnp.log(safe), NEG_FILL)
    out = acc / safe[..., None]
    packed = jnp.stack((out, jnp.broadcast_to(lse[..., None], out.shape)), axis=1)
    packed = packed.reshape((size, row_count, 2) + out.shape[1:])
    remote = lax.all_to_all(packed, "ctx", split_axis=0, concat_axis=0, tiled=True)

    owned = lax.dynamic_slice_in_dim(projected, ctx_index * row_count, row_count, 0)
    owned_q = owned[:, :q_width].reshape(tok_dev, 2, kv_local, group, HEAD_SIZE)
    fresh_keys = projected[:, q_width : q_width + k_width].reshape(
        resp_tokens, 2, kv_local, HEAD_SIZE
    )
    fresh_values = projected[:, q_width + k_width :].reshape(resp_tokens, 2, kv_local, HEAD_SIZE)
    self_scores = (
        jnp.einsum("trgjd,urgd->trgju", owned_q, fresh_keys, preferred_element_type=jnp.float32)
        * scale
    )
    token_pos = ctx_index * tok_dev + lax.iota(jnp.int32, tok_dev)
    key_pos = lax.iota(jnp.int32, resp_tokens)
    self_live = (key_pos[None, None, :] <= token_pos[:, None, None]) & (
        key_pos[None, None, :] < resp_len[None, :, None]
    )
    self_live = self_live[:, :, None, None, :]
    self_scores = jnp.where(self_live, self_scores, NEG_FILL)
    self_peak = jnp.max(self_scores, axis=-1)
    self_weights = jnp.where(self_live, jnp.exp(self_scores - self_peak[..., None]), 0.0)
    self_total = jnp.sum(self_weights, axis=-1)
    self_acc = jnp.einsum(
        "trgju,urgd->trgjd",
        self_weights.astype(jnp.bfloat16),
        fresh_values,
        preferred_element_type=jnp.float32,
    )
    flat = (row_count, kv_local, group)
    self_peak = self_peak.reshape(flat)
    self_total = self_total.reshape(flat)
    self_acc = self_acc.reshape(flat + (HEAD_SIZE,))

    remote_out = remote[:, :, 0]
    remote_lse = remote[:, :, 1]
    overall = jnp.maximum(jnp.max(remote_lse, axis=0), self_peak[..., None])
    remote_weight = jnp.exp(remote_lse - overall)
    self_factor = jnp.exp(self_peak[..., None] - overall)
    numerator = jnp.sum(remote_weight * remote_out, axis=0) + self_factor * self_acc
    denominator = jnp.sum(remote_weight, axis=0) + self_factor * self_total[..., None]
    result = numerator / denominator
    row_live = (token_pos[:, None] < resp_len[None, :]).reshape(row_count)
    result = jnp.where(row_live[:, None, None, None], result, 0.0)
    return result.reshape(tok_dev, 2, q_width).astype(jnp.bfloat16)


def solution(mesh):
    return jax.shard_map(
        shards,
        mesh=mesh,
        in_specs=(
            P(("pairs", "ctx"), None, None),
            P("ctx", "head"),
            P(None, "ctx", "head"),
            P("head"),
            P(None, "head"),
            P(None, ("pairs", "ctx"), "head"),
            P("pairs"),
            P("pairs"),
        ),
        out_specs=P(("pairs", "ctx"), None, "head"),
        check_vma=False,
    )
```

time: 206 us -> 60.2 us (0.29)
  waiting for transfers between devices: 90.1 us -> 24.5 us
  other arithmetic: 46.9 us -> 3.38 us
  local copies, waits for them, and re-layouts: 31 us -> 12.1 us
  between operations: 14.3 us -> 0.84 us
  starting transfers between devices: 18.4 us -> 12.4 us
    psum x1 -> x0, waiting for transfers between devices: 67.2 us -> none  [shards(): lax.psum(jnp.dot(flat_rows, weights_all, preferred_element_type=jnp.float...]
    unnamed x1 -> x0, other arithmetic: 45.3 us -> none
    ppermute x0 -> x3, waiting for transfers between devices: none -> 13.8 us  [sum_over(): other = lax.ppermute(value.astype(jnp.bfloat16), axis, pairs)]
    all_to_all x4 -> x2, waiting for transfers between devices: 22.9 us -> 10.7 us  [the longest x1 7.42 us: shards(): lax.all_to_all(packed, 'ctx', split_axis=0, concat_axis=0, tiled=True)]
    unnamed x18 -> x16, local copies, waits for them, and re-layouts: 19.2 us -> 9.32 us
    all_to_all x2 -> x0, local copies, waits for them, and re-layouts: 8.11 us -> none  [shards(): lax.all_to_all(hidden, 'ctx', split_axis=2, concat_axis=0, tiled=True)]
    all_to_all x4 -> x2, starting transfers between devices: 18.4 us -> 10.7 us  [the longest x1 7.28 us: shards(): lax.all_to_all(sent, 'ctx', split_axis=0, concat_axis=0, tiled=True)]
    dot_general x5 -> x7, matrix products: 4.29 us -> 6.28 us  [the longest x1 2.85 us: shards(): jnp.dot(flat_rows, wq, preferred_element_type=jnp.float32)]
  transfers between devices with their start and end apart: 5 -> 5, of which waited for: 5 -> 5; matrix products, arithmetic and copies ran while one was open for 2% -> 6% of each run, Pallas kernels for 0% -> 0%
where the time goes in v1:
time: 60.2 us; the launch traced here: 59.5 us
  waiting for transfers between devices  24.5 us (41%)
  starting transfers between devices  12.4 us (21%)
  local copies, waits for them, and re-layouts  12.1 us (20%)
  matrix products  6.28 us (10%)
  other arithmetic  3.38 us (6%)
  between operations  0.84 us (1%)
    ppermute x3, waiting for transfers between devices, sum_over(): other = lax.ppermute(value.astype(jnp.bfloat16), axis, pairs)  13.8 us
    unnamed x16, local copies, waits for them, and re-layouts  9.32 us
    all_to_all x1, waiting for transfers between devices, shards(): lax.all_to_all(packed, 'ctx', split_axis=0, concat_axis=0, tiled=True)  7.42 us
    all_to_all x1, starting transfers between devices, shards(): lax.all_to_all(sent, 'ctx', split_axis=0, concat_axis=0, tiled=True)  7.28 us
    all_to_all x1, starting transfers between devices, shards(): lax.all_to_all(packed, 'ctx', split_axis=0, concat_axis=0, tiled=True)  3.41 us
    all_to_all x1, waiting for transfers between devices, shards(): lax.all_to_all(sent, 'ctx', split_axis=0, concat_axis=0, tiled=True)  3.27 us
    dot_general x1, matrix products, shards(): jnp.dot(flat_rows, wq, preferred_element_type=jnp.float32)  2.85 us
    ppermute x3, starting transfers between devices, sum_over(): other = lax.ppermute(value.astype(jnp.bfloat16), axis, pairs)  1.71 us
  transfers between devices with their start and end apart: 5, of which 5 were waited for; matrix products, arithmetic and copies ran while one was open for 6% of the time, Pallas kernels for 0%

profile of v1, /device:TPU:0, one launch (start us, length us, event | category | flops | bytes accessed | tf_op | source)
XLA Modules:
  0.0 59.5 jit_solution(6519000334209719559)
XLA Ops:
  0.0 0.0 copy-start.1
  0.0 1.3 %constant_dynamic-update-slice_fusion.7 = bf16[8,2,1024]{2,1,0:T(2,128)(2,1)} fusion(bf16[2,8192]{1,0:T(2,128)(2,1)} %bitcast.128), kind=kLoop, calls=%fused_computation.49 | loop fusion | bytes 8192
  1.3 1.3 %constant_dynamic-update-slice_fusion.6 = bf16[8,2,1024]{2,1,0:T(2,128)(2,1)} fusion(bf16[8,2,1024]{2,1,0:T(2,128)(2,1)} %constant_dynamic-update-slice_fusion.7, bf16[2,8192]{1,0:T(2,128)(2,1)} %bitcast.129), kind=kLoop, calls=%fused_computation.48 | loop fusion | bytes 8192
  2.6 0.0 copy-start
  2.6 1.3 %constant_dynamic-update-slice_fusion.5 = bf16[8,2,1024]{2,1,0:T(2,128)(2,1)} fusion(bf16[8,2,1024]{2,1,0:T(2,128)(2,1)} %constant_dynamic-update-slice_fusion.6, bf16[2,8192]{1,0:T(2,128)(2,1)} %bitcast.130), kind=kLoop, calls=%fused_computation.47 | loop fusion | bytes 8192
  3.9 1.3 %constant_dynamic-update-slice_fusion.4 = bf16[8,2,1024]{2,1,0:T(2,128)(2,1)} fusion(bf16[8,2,1024]{2,1,0:T(2,128)(2,1)} %constant_dynamic-update-slice_fusion.5, bf16[2,8192]{1,0:T(2,128)(2,1)} %bitcast.131), kind=kLoop, calls=%fused_computation.46 | loop fusion | bytes 8192
  5.2 1.3 %constant_dynamic-update-slice_fusion.3 = bf16[8,2,1024]{2,1,0:T(2,128)(2,1)} fusion(bf16[8,2,1024]{2,1,0:T(2,128)(2,1)} %constant_dynamic-update-slice_fusion.4, bf16[2,8192]{1,0:T(2,128)(2,1)} %bitcast.132), kind=kLoop, calls=%fused_computation.45 | loop fusion | bytes 8192
  6.4 1.3 %constant_dynamic-update-slice_fusion.2 = bf16[8,2,1024]{2,1,0:T(2,128)(2,1)} fusion(bf16[8,2,1024]{2,1,0:T(2,128)(2,1)} %constant_dynamic-update-slice_fusion.3, bf16[2,8192]{1,0:T(2,128)(2,1)} %bitcast.133), kind=kLoop, calls=%fused_computation.44 | loop fusion | bytes 8192
  7.7 1.3 %constant_dynamic-update-slice_fusion.1 = bf16[8,2,1024]{2,1,0:T(2,128)(2,1)} fusion(bf16[8,2,1024]{2,1,0:T(2,128)(2,1)} %constant_dynamic-update-slice_fusion.2, bf16[2,8192]{1,0:T(2,128)(2,1)} %bitcast.134), kind=kLoop, calls=%fused_computation.43 | loop fusion | bytes 8192
  9.0 1.3 %constant_dynamic-update-slice_fusion = bf16[8,2,1024]{2,1,0:T(2,128)(2,1)} fusion(bf16[8,2,1024]{2,1,0:T(2,128)(2,1)} %constant_dynamic-update-slice_fusion.1, bf16[2,8192]{1,0:T(2,128)(2,1)} %bitcast.135), kind=kLoop, calls=%fused_computation.42 | loop fusion | bytes 8192 | tf_op jit(solution)/shard_map/stack | solution.py:13
  10.3 7.3 %all-to-all-start = ((bf16[8,2,1024]{2,1,0:T(2,128)(2,1)}), bf16[8,2,1024]{2,1,0:T(2,128)(2,1)S(1)}, u32[]{:S(2)}, u32[]{:S(2)}) async-start(bf16[8,2,1024]{2,1,0:T(2,128)(2,1)} %constant_dynamic-update-slice_fusion), calls=%async_computation | async-start | bytes 65536 | tf_op jit(solution)/shard_map/all_to_all | solution.py:41
  17.6 1.1 %fusion.42 = (bf16[1,512,256]{2,1,0:T(8,128)(2,1)S(1)}, bf16[1,512,256]{2,1,0:T(8,128)(2,1)S(1)}) fusion(bf16[2,512,256]{2,1,0:T(8,128)(2,1)} %param.13), kind=kLoop, calls=%fused_computation.86 | loop fusion | bytes 1048576 | tf_op jit(solution)/shard_map/slice | solution.py:57
  18.6 0.7 %compare_and_fusion = pred[2,8]{1,0:T(4,128)(4,1)S(1)} fusion(pred[8]{0:T(512)(128)(4,1)S(1)} %iota_compare_fusion, s32[2]{0:T(128)} %param.15), kind=kLoop, calls=%fused_computation.78 | loop fusion | flops 32 | bytes 32 | tf_op jit(solution)/shard_map/and | solution.py:87
  19.4 0.7 %broadcast_compare_fusion = pred[2]{0:T(512)(128)(4,1)S(1)} fusion(s32[2]{0:T(128)} %param.15, s32[]{:T(128)S(6)} %axis_index.15), kind=kLoop, calls=%fused_computation.82 | loop fusion | flops 2 | bytes 14 | tf_op jit(solution)/shard_map/lt | solution.py:114
  20.7 0.1 copy.71
  20.8 0.1 copy.72
  21.0 3.3 %all-to-all-done = bf16[8,2,1024]{2,1,0:T(2,128)(2,1)S(1)} async-done(((bf16[8,2,1024]{2,1,0:T(2,128)(2,1)}), bf16[8,2,1024]{2,1,0:T(2,128)(2,1)S(1)}, u32[]{:S(2)}, u32[]{:S(2)}) %all-to-all-start) | async-done | bytes 32800 | tf_op jit(solution)/shard_map/all_to_all | solution.py:41
  24.3 1.2 %fusion.6 = f32[16,256]{1,0:T(8,128)S(1)} fusion(bf16[16,1024]{1,0:T(8,128)(2,1)S(1)} %reshape.246, bf16[2,1024,256]{2,1,0:T(8,128)(2,1)} %param.10), kind=kOutput, calls=%fused_computation.10 | convolution fusion | flops 8388608 | bytes 573440 | tf_op jit(solution)/shard_map/dot_general | solution.py:47
  25.5 1.2 %fusion.8 = f32[16,256]{1,0:T(8,128)S(1)} fusion(bf16[16,1024]{1,0:T(8,128)(2,1)S(1)} %reshape.246, bf16[2,1024,256]{2,1,0:T(8,128)(2,1)} %param.10), kind=kOutput, calls=%fused_computation.12 | convolution fusion | flops 8388608 | bytes 573440 | tf_op jit(solution)/shard_map/dot_general | solution.py:46
  26.7 2.9 %fusion.46 = f32[16,2048]{1,0:T(8,128)S(1)} fusion(bf16[16,1024]{1,0:T(8,128)(2,1)S(1)} %reshape.246, bf16[1024,2048]{1,0:T(8,128)(2,1)} %param.9), kind=kOutput, calls=%fused_computation.90 | convolution fusion | flops 67108864 | bytes 4358144 | tf_op jit(solution)/shard_map/dot_general | solution.py:45
  29.6 0.5 collective-permute-start
  30.1 0.0 copy-done.1
  30.2 3.9 %collective-permute-done = bf16[16,2560]{1,0:T(8,128)(2,1)S(1)} collective-permute-done((bf16[16,2560]{1,0:T(8,128)(2,1)S(1)}, bf16[16,2560]{1,0:T(8,128)(2,1)S(1)}, u32[]{:S(2)}, u32[]{:S(2)}) %collective-permute-start) | collective-permute-done | bytes 81952 | tf_op jit(solution)/shard_map/ppermute | solution.py:21
  34.1 0.5 collective-permute-start.1
  34.6 0.0 copy-done
  34.6 4.3 %collective-permute-done.1 = bf16[16,2560]{1,0:T(8,128)(2,1)S(1)} collective-permute-done((bf16[16,2560]{1,0:T(8,128)(2,1)S(1)}, bf16[16,2560]{1,0:T(8,128)(2,1)S(1)}, u32[]{:S(2)}, u32[]{:S(2)}) %collective-permute-start.1) | collective-permute-done | bytes 81952 | tf_op jit(solution)/shard_map/ppermute | solution.py:21
  39.0 0.7 %collective-permute-start.2 = (bf16[16,2560]{1,0:T(8,128)(2,1)S(1)}, bf16[16,2560]{1,0:T(8,128)(2,1)S(1)}, u32[]{:S(2)}, u32[]{:S(2)}) collective-permute-start(bf16[16,2560]{1,0:T(8,128)(2,1)S(1)} %fusion.22), channel_id=1, source_target_pairs={{0,8},{2,10},{4,12},{6,14},{8,0},{10,2},{12,4},{14,6},{1,9},{3,11}... | collective-permute-start | bytes 245768 | tf_op jit(solution)/shard_map/ppermute | solution.py:21
  39.7 5.6 %collective-permute-done.2 = bf16[16,2560]{1,0:T(8,128)(2,1)S(1)} collective-permute-done((bf16[16,2560]{1,0:T(8,128)(2,1)S(1)}, bf16[16,2560]{1,0:T(8,128)(2,1)S(1)}, u32[]{:S(2)}, u32[]{:S(2)}) %collective-permute-start.2) | collective-permute-done | bytes 81952 | tf_op jit(solution)/shard_map/ppermute | solution.py:21
  45.3 0.3 fusion.44
  45.6 0.2 fusion.12
  45.9 0.3 fusion.2
  46.2 0.1 stack_broadcast_in_dim.2
  46.3 0.7 %pad_maximum_fusion = f32[8,2,2,2,8,128]{5,4,1,3,2,0:T(8,128)} fusion(f32[8,2,1,2,8,128]{5,4,1,3,2,0:T(8,128)S(1)} %stack_broadcast_in_dim.2, f32[8,2,1,2,8,128]{5,4,1,0,3,2:T(8,128)S(1)} %bitcast.127), kind=kLoop, calls=%fused_computation.19 | loop fusion | flops 65536 | bytes 524288 | tf_op jit(solution)/shard_map/stack | solution.py:71
  47.0 3.4 %all-to-all-start.1 = ((f32[8,2,2,2,8,128]{5,4,1,3,2,0:T(8,128)}), f32[8,2,2,2,8,128]{5,4,1,3,2,0:T(8,128)S(1)}, u32[]{:S(2)}, u32[]{:S(2)}) async-start(f32[8,2,2,2,8,128]{5,4,1,3,2,0:T(8,128)} %pad_maximum_fusion), calls=%async_computation.1 | async-start | bytes 524288 | tf_op jit(solution)/shard_map/all_to_all | solution.py:73
  50.5 0.1 fusion.45
  50.7 0.3 convolution_bitcast_fusion.1
  50.9 0.1 fusion.28
  51.0 0.1 mul.64
  51.1 0.1 max.24.clone
  51.2 7.4 %all-to-all-done.1 = f32[8,2,2,2,8,128]{5,4,1,3,2,0:T(8,128)S(1)} async-done(((f32[8,2,2,2,8,128]{5,4,1,3,2,0:T(8,128)}), f32[8,2,2,2,8,128]{5,4,1,3,2,0:T(8,128)S(1)}, u32[]{:S(2)}, u32[]{:S(2)}) %all-to-all-start.1) | async-done | bytes 262176 | tf_op jit(solution)/shard_map/all_to_all | solution.py:73
  58.6 0.1 broadcast_maximum_fusion
  58.8 0.7 %select_convert_fusion = bf16[1,2,2048]{2,1,0:T(2,128)(2,1)} fusion(pred[2]{0:T(512)(128)(4,1)S(1)} %broadcast_compare_fusion, f32[1,2,2048]{2,1,0:T(2,128)S(1)} %reduce_sum.47, f32[1,2,2048]{2,1,0:T(2,128)S(1)} %mul.65, f32[1,2,2048]{2,1,0:T(2,128)S(1)} %reduce_sum.45, f32[1,2,2048]{2,1,0:T(2,128)S(1)} %reshape.252, f32[1,2,2048]{2,1,0:T(2,128)S(1)} %max.26, ...), kind=kLoop, calls=%fused_computation.53 | loop fusion | flops 36864 | bytes 106498 | tf_op jit(solution)/shard_map/convert_element_type | solution.py:116
  (29 shorter events, 0.4 us)
Async XLA Ops:
  0.0 30.1 %copy-start.1 = (bf16[2,256]{1,0:T(2,128)(2,1)S(1)}, bf16[2,256]{1,0:T(2,128)(2,1)}, u32[]{:S(2)}) copy-start(bf16[2,256]{1,0:T(2,128)(2,1)} %param.12) | copy-start | bytes 3076
  2.6 32.0 %copy-start = (bf16[2048]{0:T(1024)(128)(2,1)S(1)}, bf16[2048]{0:T(1024)(128)(2,1)}, u32[]{:S(2)}) copy-start(bf16[2048]{0:T(1024)(128)(2,1)} %param.11) | copy-start | bytes 12292
  10.3 14.0 %all-to-all-start = ((bf16[8,2,1024]{2,1,0:T(2,128)(2,1)}), bf16[8,2,1024]{2,1,0:T(2,128)(2,1)S(1)}, u32[]{:S(2)}, u32[]{:S(2)}) async-start(bf16[8,2,1024]{2,1,0:T(2,128)(2,1)} %constant_dynamic-update-slice_fusion), calls=%async_computation | async-start | bytes 65536 | tf_op jit(solution)/shard_map/all_to_all | solution.py:41
  29.6 4.5 %collective-permute-start = (bf16[16,2560]{1,0:T(8,128)(2,1)S(1)}, bf16[16,2560]{1,0:T(8,128)(2,1)S(1)}, u32[]{:S(2)}, u32[]{:S(2)}) collective-permute-start(bf16[16,2560]{1,0:T(8,128)(2,1)S(1)} %fusion.21), channel_id=1, source_target_pairs={{0,2},{2,0},{4,6},{6,4},{8,10},{10,8},{12,14},{14,12},{1,3},{3,1},... | collective-permute-start | bytes 245768 | tf_op jit(solution)/shard_map/ppermute | solution.py:21
  34.1 4.8 %collective-permute-start.1 = (bf16[16,2560]{1,0:T(8,128)(2,1)S(1)}, bf16[16,2560]{1,0:T(8,128)(2,1)S(1)}, u32[]{:S(2)}, u32[]{:S(2)}) collective-permute-start(bf16[16,2560]{1,0:T(8,128)(2,1)S(1)} %fusion.41), channel_id=1, source_target_pairs={{0,4},{2,6},{4,0},{6,2},{8,12},{10,14},{12,8},{14,10},{1,5},{3,7},... | collective-permute-start | bytes 245768 | tf_op jit(solution)/shard_map/ppermute | solution.py:21
  39.0 6.3 %collective-permute-start.2 = (bf16[16,2560]{1,0:T(8,128)(2,1)S(1)}, bf16[16,2560]{1,0:T(8,128)(2,1)S(1)}, u32[]{:S(2)}, u32[]{:S(2)}) collective-permute-start(bf16[16,2560]{1,0:T(8,128)(2,1)S(1)} %fusion.22), channel_id=1, source_target_pairs={{0,8},{2,10},{4,12},{6,14},{8,0},{10,2},{12,4},{14,6},{1,9},{3,11}... | collective-permute-start | bytes 245768 | tf_op jit(solution)/shard_map/ppermute | solution.py:21
  47.0 11.6 %all-to-all-start.1 = ((f32[8,2,2,2,8,128]{5,4,1,3,2,0:T(8,128)}), f32[8,2,2,2,8,128]{5,4,1,3,2,0:T(8,128)S(1)}, u32[]{:S(2)}, u32[]{:S(2)}) async-start(f32[8,2,2,2,8,128]{5,4,1,3,2,0:T(8,128)} %pad_maximum_fusion), calls=%async_computation.1 | async-start | bytes 524288 | tf_op jit(solution)/shard_map/all_to_all | solution.py:73

commit v2 on v1

v2 whole, which is shorter than its diff:
```python
import functools

import jax
import jax.numpy as jnp
from jax import lax
from jax.experimental import pallas as pl
from jax.experimental.pallas import tpu as pltpu
from jax.sharding import PartitionSpec as P

HEAD_SIZE = 128
NEG_FILL = -1e30
MIB = 2**20
STAT_ROWS = 16
PROJECT_LIMIT = 53 * MIB

ANY = pl.BlockSpec(memory_space=pl.ANY)
VMEM = pl.BlockSpec(memory_space=pltpu.VMEM)
SMEM = pl.BlockSpec(memory_space=pltpu.SMEM)


def project_kernel(pieces, rows_ref, wq, wkv, out_ref, wq_here, wkv_here, sems):
    width = wq.shape[1] // pieces
    k_width = wkv.shape[2]
    copies = [
        pltpu.make_async_copy(wq.at[:, pl.ds(i * width, width)], wq_here.at[i], sems.at[i])
        for i in range(pieces)
    ]
    copies += [
        pltpu.make_async_copy(wkv.at[i], wkv_here.at[i], sems.at[pieces + i]) for i in range(2)
    ]
    for copy in copies:
        copy.start()
    if len(rows_ref.shape) == 3:
        rows = jnp.concatenate([rows_ref[i] for i in range(rows_ref.shape[0])], axis=0)
    else:
        rows = rows_ref[...]
    for i in range(pieces):
        copies[i].wait()
        out_ref[:, i * width : (i + 1) * width] = jnp.dot(
            rows, wq_here[i], preferred_element_type=jnp.float32
        )
    for i in range(2):
        copies[pieces + i].wait()
        first = pieces * width + i * k_width
        out_ref[:, first : first + k_width] = jnp.dot(
            rows, wkv_here[i], preferred_element_type=jnp.float32
        )


def project(rows, wq, wkv, pieces):
    depth, q_width = wq.shape
    width = q_width + 2 * wkv.shape[2]
    return pl.pallas_call(
        functools.partial(project_kernel, pieces),
        out_shape=jax.ShapeDtypeStruct((rows.size // depth, width), jnp.float32),
        in_specs=[VMEM, ANY, ANY],
        out_specs=VMEM,
        scratch_shapes=[
            pltpu.VMEM((pieces, depth, q_width // pieces), wq.dtype),
            pltpu.VMEM(wkv.shape, wkv.dtype),
            pltpu.SemaphoreType.DMA((pieces + 2,)),
        ],
        compiler_params=pltpu.CompilerParams(vmem_limit_bytes=PROJECT_LIMIT),
        name="project",
    )(rows, wq, wkv)


def attend_kernel(kv_local, group, tok_dev, place, limits, query, fresh, cache, out):
    rows = fresh.shape[1]
    size = out.shape[0]
    own = query.shape[1] // size
    cache_len = cache.shape[1]
    scale = HEAD_SIZE ** (-0.5)
    first_slot = place[0] * cache_len
    first_row = place[0] * 2 * tok_dev
    long = (query.shape[1], cache_len)
    live = first_slot + lax.broadcasted_iota(jnp.int32, long, 1) < limits[0]
    short = (query.shape[1], rows)
    row = lax.broadcasted_iota(jnp.int32, short, 0) // group
    key = lax.broadcasted_iota(jnp.int32, short, 1)
    mine = (row >= first_row) & (row < first_row + 2 * tok_dev)
    filled = jnp.where(key % 2 == 0, limits[1], limits[2])
    seen = mine & (key % 2 == row % 2) & (key // 2 <= row // 2) & (key // 2 < filled)
    lane = lax.broadcasted_iota(jnp.int32, (own, HEAD_SIZE), 1)
    place_in_owner = lax.broadcasted_iota(jnp.int32, (own, HEAD_SIZE), 0)
    contract = (((1,), (1,)), ((), ()))
    stats = jnp.zeros((size, HEAD_SIZE), jnp.float32)
    for g in range(kv_local):
        heads = slice(g * HEAD_SIZE, (g + 1) * HEAD_SIZE)
        q = query[g]
        scores = scale * lax.dot_general(
            q, cache[0, :, heads], contract, preferred_element_type=jnp.float32
        )
        scores = jnp.where(live, scores, NEG_FILL)
        near = scale * lax.dot_general(
            q, fresh[0, :, heads], contract, preferred_element_type=jnp.float32
        )
        near = jnp.where(seen, near, NEG_FILL)
        peak = jnp.maximum(
            jnp.max(scores, axis=1, keepdims=True), jnp.max(near, axis=1, keepdims=True)
        )
        weights = jnp.where(live, jnp.exp(scores - peak), 0.0)
        near_weights = jnp.where(seen, jnp.exp(near - peak), 0.0)
        total = jnp.sum(weights, axis=1, keepdims=True) + jnp.sum(
            near_weights, axis=1, keepdims=True
        )
        acc = jnp.dot(
            weights.astype(jnp.bfloat16), cache[1, :, heads], preferred_element_type=jnp.float32
        )
        acc = acc + jnp.dot(
            near_weights.astype(jnp.bfloat16),
            fresh[1, :, heads],
            preferred_element_type=jnp.float32,
        )
        some = total > 0.0
        safe = jnp.where(some, total, 1.0)
        lse = jnp.where(some, peak + jnp.log(safe), NEG_FILL)
        mean = (acc / safe).astype(jnp.bfloat16)
        out[:, g * own : (g + 1) * own, :] = mean.reshape(size, own, HEAD_SIZE)
        spread = jnp.where(
            (lane == g * own + place_in_owner)[None],
            jnp.broadcast_to(lse, (size * own, HEAD_SIZE)).reshape(size, own, HEAD_SIZE),
            0.0,
        )
        stats = stats + jnp.sum(spread, axis=1)
    high = stats.astype(jnp.bfloat16)
    rest = stats - high.astype(jnp.float32)
    middle = rest.astype(jnp.bfloat16)
    low = rest - middle.astype(jnp.float32)
    which = lax.broadcasted_iota(jnp.int32, (size, STAT_ROWS, HEAD_SIZE), 1)
    terms = jnp.where(
        which == 0,
        high.astype(jnp.float32)[:, None, :],
        jnp.where(which == 1, middle.astype(jnp.float32)[:, None, :], low[:, None, :]),
    )
    out[:, kv_local * own :, :] = terms.astype(jnp.bfloat16)


def attend(place, limits, query, fresh, cache, size, group, tok_dev):
    kv_local = query.shape[0]
    own = query.shape[1] // size
    return pl.pallas_call(
        functools.partial(attend_kernel, kv_local, group, tok_dev),
        out_shape=jax.ShapeDtypeStruct(
            (size, kv_local * own + STAT_ROWS, HEAD_SIZE), jnp.bfloat16
        ),
        in_specs=[SMEM, SMEM, VMEM, VMEM, VMEM],
        out_specs=VMEM,
        compiler_params=pltpu.CompilerParams(
            vmem_limit_bytes=8 * MIB if query.shape[1] <= 512 else 48 * MIB
        ),
        name="attend",
    )(place, limits, query, fresh, cache)


def combine_kernel(kv_local, group, tok_dev, place, limits, parts, out):
    count = out.shape[0]
    own = count // kv_local
    stats = (
        parts[:, count, :].astype(jnp.float32)
        + parts[:, count + 1, :].astype(jnp.float32)
        + parts[:, count + 2, :].astype(jnp.float32)
    )
    peak = jnp.max(stats, axis=0, keepdims=True)
    weights = jnp.exp(stats - peak)
    weights = weights / jnp.sum(weights, axis=0, keepdims=True)
    lane = lax.broadcasted_iota(jnp.int32, (1, HEAD_SIZE), 1)
    row = (lane % own) // group
    filled = jnp.where(row % 2 == 0, limits[1], limits[2])
    weights = jnp.where(place[0] * tok_dev + row // 2 < filled, weights, 0.0)
    mask = lax.broadcasted_iota(jnp.int32, (count, HEAD_SIZE), 0) == lax.broadcasted_iota(
        jnp.int32, (count, HEAD_SIZE), 1
    )
    spread = jnp.where(mask[None], weights[:, None, :], 0.0)
    column = jnp.sum(spread, axis=2, keepdims=True)
    out[...] = jnp.sum(column * parts[:, :count, :].astype(jnp.float32), axis=0)


def combine(place, limits, parts, kv_local, group, tok_dev):
    count = parts.shape[1] - STAT_ROWS
    return pl.pallas_call(
        functools.partial(combine_kernel, kv_local, group, tok_dev),
        out_shape=jax.ShapeDtypeStruct((count, HEAD_SIZE), jnp.float32),
        in_specs=[SMEM, SMEM, VMEM],
        out_specs=VMEM,
        compiler_params=pltpu.CompilerParams(vmem_limit_bytes=8 * MIB),
        name="combine",
    )(place, limits, parts)


def sum_over(value, axis, size):
    bit = 1
    while bit < size:
        pairs = [(d, d ^ bit) for d in range(size)]
        other = lax.ppermute(value.astype(jnp.bfloat16), axis, pairs)
        value = value + other.astype(jnp.float32)
        bit *= 2
    return value


def shards(hidden, wq, wkv, bias_q, bias_kv, key_value_cache, prompt_len, resp_len):
    tok_dev = hidden.shape[0]
    size = lax.axis_size("ctx")
    ctx_index = lax.axis_index("ctx")
    q_width = wq.shape[1]
    k_width = wkv.shape[2]
    kv_local = k_width // HEAD_SIZE
    group = q_width // k_width
    row_count = 2 * tok_dev
    rows = row_count * size
    place = ctx_index.astype(jnp.int32).reshape(1)
    limits = jnp.concatenate((prompt_len, resp_len))

    sent = hidden.reshape(row_count, size, hidden.shape[2] // size)
    columns = lax.all_to_all(sent, "ctx", split_axis=1, concat_axis=1, tiled=True)
    columns = jnp.swapaxes(columns, 0, 1)
    if size > 16:
        columns = columns.reshape(rows, columns.shape[2])
    partial = project(columns, wq, wkv, 4)
    bias_all = jnp.concatenate((bias_q, bias_kv[0], bias_kv[1])).astype(jnp.float32)
    projected = (sum_over(partial, "ctx", size) + bias_all).astype(jnp.bfloat16)
    query = projected[:, :q_width].reshape(rows, kv_local, group, HEAD_SIZE)
    query = jnp.transpose(query, (1, 0, 2, 3)).reshape(kv_local, rows * group, HEAD_SIZE)
    fresh = jnp.stack(
        (projected[:, q_width : q_width + k_width], projected[:, q_width + k_width :])
    )
    parts = attend(place, limits, query, fresh, key_value_cache, size, group, tok_dev)
    parts = lax.all_to_all(parts, "ctx", split_axis=0, concat_axis=0, tiled=True)
    result = combine(place, limits, parts, kv_local, group, tok_dev)
    result = result.reshape(kv_local, row_count, group, HEAD_SIZE)
    result = jnp.transpose(result, (1, 0, 2, 3))
    return result.reshape(tok_dev, 2, q_width).astype(jnp.bfloat16)


def solution(mesh):
    return jax.shard_map(
        shards,
        mesh=mesh,
        in_specs=(
            P(("pairs", "ctx"), None, None),
            P("ctx", "head"),
            P(None, "ctx", "head"),
            P("head"),
            P(None, "head"),
            P(None, ("pairs", "ctx"), "head"),
            P("pairs"),
            P("pairs"),
        ),
        out_specs=P(("pairs", "ctx"), None, "head"),
        check_vma=False,
    )
```

time: 60.2 us -> 45.4 us (0.75)
  local copies, waits for them, and re-layouts: 12.1 us -> 0.68 us
  blocking collectives: 0 us -> 9.51 us
  matrix products: 6.28 us -> 0 us
  Pallas kernels: 0 us -> 5.02 us
  waiting for transfers between devices: 24.5 us -> 19.8 us
  starting transfers between devices: 12.4 us -> 9.15 us
  other arithmetic: 3.38 us -> 0.21 us
    all_to_all x0 -> x1, blocking collectives: none -> 9.51 us  [shards(): lax.all_to_all(parts, 'ctx', split_axis=0, concat_axis=0, tiled=True)]
    unnamed x16 -> x10, local copies, waits for them, and re-layouts: 9.32 us -> 0.03 us
    dot_general x7 -> x0, matrix products: 6.28 us -> none  [the longest x1 2.85 us: shards(): jnp.dot(flat_rows, wq, preferred_element_type=jnp.float32)]
    pallas_call x0 -> x3, Pallas kernels: none -> 5.02 us  [the longest x1 3 us: project(): pl.pallas_call(functools.partial(project_kernel, pieces), out_shape=jax.S...]
    all_to_all x2 -> x1, waiting for transfers between devices: 10.7 us -> 6.03 us  [shards(): lax.all_to_all(sent, 'ctx', split_axis=1, concat_axis=1, tiled=True)]
    all_to_all x2 -> x1, starting transfers between devices: 10.7 us -> 7.44 us  [shards(): lax.all_to_all(sent, 'ctx', split_axis=1, concat_axis=1, tiled=True)]
    another operation x2 -> x1, local copies, waits for them, and re-layouts: 1.37 us -> 0.01 us  [shards(): jnp.stack((projected[:, q_width:q_width + k_width], projected[:, q_width...]
    slice x2 -> x0, local copies, waits for them, and re-layouts: 1.07 us -> none  [the longest x1 1.07 us: shards(): values = key_value_cache[1].reshape(cache_len, kv_local, HEAD_SIZE)]
  transfers between devices with their start and end apart: 5 -> 4, of which waited for: 5 -> 4; matrix products, arithmetic and copies ran while one was open for 6% -> 0% of each run, Pallas kernels for 0% -> 0%
where the time goes in v2:
time: 45.4 us; the launch traced here: 45.1 us
  waiting for transfers between devices  19.8 us (44%)
  blocking collectives  9.51 us (21%)
  starting transfers between devices  9.15 us (20%)
  Pallas kernels  5.02 us (11%)
  between operations  0.76 us (2%)
  local copies, waits for them, and re-layouts  0.68 us (1%)
    ppermute x3, waiting for transfers between devices, sum_over(): other = lax.ppermute(value.astype(jnp.bfloat16), axis, pairs)  13.8 us
    all_to_all x1, blocking collectives, shards(): lax.all_to_all(parts, 'ctx', split_axis=0, concat_axis=0, tiled=True)  9.51 us
    all_to_all x1, starting transfers between devices, shards(): lax.all_to_all(sent, 'ctx', split_axis=1, concat_axis=1, tiled=True)  7.44 us
    all_to_all x1, waiting for transfers between devices, shards(): lax.all_to_all(sent, 'ctx', split_axis=1, concat_axis=1, tiled=True)  6.03 us
    pallas_call x1, Pallas kernels, project(): pl.pallas_call(functools.partial(project_kernel, pieces), out_shape=jax.S...  3 us
    ppermute x3, starting transfers between devices, sum_over(): other = lax.ppermute(value.astype(jnp.bfloat16), axis, pairs)  1.71 us
    pallas_call x1, Pallas kernels, attend(): pl.pallas_call(functools.partial(attend_kernel, kv_local, group, tok_dev)...  1.34 us
  transfers between devices with their start and end apart: 4, of which 4 were waited for; matrix products, arithmetic and copies ran while one was open for 0% of the time, Pallas kernels for 0%

profile of v2, /device:TPU:0, one launch (start us, length us, event | category | flops | bytes accessed | tf_op | source)
XLA Modules:
  0.0 45.1 jit_solution(8403514013290445345)
XLA Ops:
  0.0 0.0 copy-start.2
  0.0 0.0 copy-start.1
  0.0 0.0 copy-start.3
  0.0 0.0 copy-start
  0.0 7.4 %all-to-all-start = ((bf16[2,8,1024]{2,0,1:T(2,128)(2,1)}), bf16[2,8,1024]{2,0,1:T(2,128)(2,1)S(1)}, u32[]{:S(2)}, u32[]{:S(2)}) async-start(bf16[2,8,1024]{2,0,1:T(2,128)(2,1)} %bitcast.25), calls=%async_computation | async-start | bytes 65536 | tf_op jit(solution)/shard_map/all_to_all | solution.py:215
  8.1 6.0 %all-to-all-done = bf16[2,8,1024]{2,0,1:T(2,128)(2,1)S(1)} async-done(((bf16[2,8,1024]{2,0,1:T(2,128)(2,1)}), bf16[2,8,1024]{2,0,1:T(2,128)(2,1)S(1)}, u32[]{:S(2)}, u32[]{:S(2)}) %all-to-all-start) | async-done | bytes 32800 | tf_op jit(solution)/shard_map/all_to_all | solution.py:215
  14.1 3.0 %project.1 = f32[16,2560]{1,0:T(8,128)S(1)} custom-call(bf16[8,2,1024]{2,1,0:T(2,128)(2,1)S(1)} %bitcast.22, bf16[1024,2048]{1,0:T(8,128)(2,1)} %wq.1, bf16[2,1024,256]{2,1,0:T(8,128)(2,1)} %wkv.1), custom_call_target="tpu_custom_call" | custom-call | tf_op jit(solution)/shard_map/project/pallas_call | solution.py:53
  17.2 0.5 %collective-permute-start = (bf16[16,2560]{1,0:T(8,128)(2,1)S(1)}, bf16[16,2560]{1,0:T(8,128)(2,1)S(1)}, u32[]{:S(2)}, u32[]{:S(2)}) collective-permute-start(bf16[16,2560]{1,0:T(8,128)(2,1)S(1)} %convert_element_type.48), channel_id=1, source_target_pairs={{0,2},{2,0},{4,6},{6,4},{8,10},{10,8},{12,14},{14,12},{1,3},{3,1},... | collective-permute-start | bytes 245768 | tf_op jit(solution)/shard_map/ppermute | solution.py:195
  17.7 0.0 copy-done.2
  17.7 3.9 %collective-permute-done = bf16[16,2560]{1,0:T(8,128)(2,1)S(1)} collective-permute-done((bf16[16,2560]{1,0:T(8,128)(2,1)S(1)}, bf16[16,2560]{1,0:T(8,128)(2,1)S(1)}, u32[]{:S(2)}, u32[]{:S(2)}) %collective-permute-start) | collective-permute-done | bytes 81952 | tf_op jit(solution)/shard_map/ppermute | solution.py:195
  21.7 0.5 %collective-permute-start.1 = (bf16[16,2560]{1,0:T(8,128)(2,1)S(1)}, bf16[16,2560]{1,0:T(8,128)(2,1)S(1)}, u32[]{:S(2)}, u32[]{:S(2)}) collective-permute-start(bf16[16,2560]{1,0:T(8,128)(2,1)S(1)} %fusion), channel_id=1, source_target_pairs={{0,4},{2,6},{4,0},{6,2},{8,12},{10,14},{12,8},{14,10},{1,5},{3,7},... | collective-permute-start | bytes 245768 | tf_op jit(solution)/shard_map/ppermute | solution.py:195
  22.1 0.0 copy-done.1
  22.2 4.3 %collective-permute-done.1 = bf16[16,2560]{1,0:T(8,128)(2,1)S(1)} collective-permute-done((bf16[16,2560]{1,0:T(8,128)(2,1)S(1)}, bf16[16,2560]{1,0:T(8,128)(2,1)S(1)}, u32[]{:S(2)}, u32[]{:S(2)}) %collective-permute-start.1) | collective-permute-done | bytes 81952 | tf_op jit(solution)/shard_map/ppermute | solution.py:195
  26.5 0.7 %collective-permute-start.2 = (bf16[16,2560]{1,0:T(8,128)(2,1)S(1)}, bf16[16,2560]{1,0:T(8,128)(2,1)S(1)}, u32[]{:S(2)}, u32[]{:S(2)}) collective-permute-start(bf16[16,2560]{1,0:T(8,128)(2,1)S(1)} %fusion.1), channel_id=1, source_target_pairs={{0,8},{2,10},{4,12},{6,14},{8,0},{10,2},{12,4},{14,6},{1,9},{3,11}... | collective-permute-start | bytes 245768 | tf_op jit(solution)/shard_map/ppermute | solution.py:195
  27.2 0.0 copy-done.3
  27.2 0.1 pad_add_fusion.limits
  27.3 5.5 %collective-permute-done.2 = bf16[16,2560]{1,0:T(8,128)(2,1)S(1)} collective-permute-done((bf16[16,2560]{1,0:T(8,128)(2,1)S(1)}, bf16[16,2560]{1,0:T(8,128)(2,1)S(1)}, u32[]{:S(2)}, u32[]{:S(2)}) %collective-permute-start.2) | collective-permute-done | bytes 81952 | tf_op jit(solution)/shard_map/ppermute | solution.py:195
  32.8 0.1 add_convert_fusion
  32.9 0.0 copy-done
  32.9 1.3 %attend.1 = bf16[8,48,128]{2,1,0:T(8,128)(2,1)S(1)} custom-call(s32[1]{0:T(128)} %bitcast.place, s32[3]{0:T(128)S(1)} %pad_add_fusion.limits, bf16[2,128,128]{2,1,0:T(8,128)(2,1)S(1)} %bitcast.21, bf16[2,16,256]{2,1,0:T(8,128)(2,1)S(1)} %pad_maximum_fusion.fresh, bf16[2,512,256]{2,1,0:T(8,128)(2,1)S(1)} %copy-done), custom_call_target="tpu_custom_call" | custom-call | tf_op jit(solution)/shard_map/attend/pallas_call | solution.py:142
  34.3 9.5 %all_to_all.10.parts = bf16[8,48,128]{2,1,0:T(8,128)(2,1)S(1)} all-to-all(bf16[8,48,128]{2,1,0:T(8,128)(2,1)S(1)} %attend.1), channel_id=1, replica_groups=mesh['pairs'=2,'ctx'=8,'head'=2] {'ctx'}, dimensions={0} | all-to-all | bytes 196608 | tf_op jit(solution)/shard_map/all_to_all | solution.py:228
  43.8 0.7 %combine.1 = f32[32,128]{1,0:T(8,128)S(1)} custom-call(s32[1]{0:T(128)} %bitcast.place, s32[3]{0:T(128)S(1)} %pad_add_fusion.limits, bf16[8,48,128]{2,1,0:T(8,128)(2,1)S(1)} %all_to_all.10.parts), custom_call_target="tpu_custom_call" | custom-call | tf_op jit(solution)/shard_map/combine/pallas_call | solution.py:181
  44.5 0.6 %convert_element_type.59 = bf16[1,2,2048]{2,1,0:T(2,128)(2,1)} reshape(bf16[2,2,8,128]{3,2,1,0:T(8,128)(2,1)S(1)} %copy.10) | data formatting | bytes 16384 | tf_op jit(solution)/shard_map/convert_element_type | solution.py:232
  (12 shorter events, 0.1 us)
Async XLA Ops:
  0.0 17.7 %copy-start.2 = (bf16[2,256]{1,0:T(2,128)(2,1)S(1)}, bf16[2,256]{1,0:T(2,128)(2,1)}, u32[]{:S(2)}) copy-start(bf16[2,256]{1,0:T(2,128)(2,1)} %param.12) | copy-start | bytes 3076
  0.0 22.1 %copy-start.1 = (bf16[2048]{0:T(1024)(128)(2,1)S(1)}, bf16[2048]{0:T(1024)(128)(2,1)}, u32[]{:S(2)}) copy-start(bf16[2048]{0:T(1024)(128)(2,1)} %param.11) | copy-start | bytes 12292
  0.0 27.2 %copy-start.3 = (s32[2]{0:T(128)S(1)}, s32[2]{0:T(128)}, u32[]{:S(2)}) copy-start(s32[2]{0:T(128)} %param.15) | copy-start | bytes 28
  0.0 32.9 %copy-start = (bf16[2,512,256]{2,1,0:T(8,128)(2,1)S(1)}, bf16[2,512,256]{2,1,0:T(8,128)(2,1)}, u32[]{:S(2)}) copy-start(bf16[2,512,256]{2,1,0:T(8,128)(2,1)} %cache.1) | copy-start | bytes 1572868
  0.0 14.1 %all-to-all-start = ((bf16[2,8,1024]{2,0,1:T(2,128)(2,1)}), bf16[2,8,1024]{2,0,1:T(2,128)(2,1)S(1)}, u32[]{:S(2)}, u32[]{:S(2)}) async-start(bf16[2,8,1024]{2,0,1:T(2,128)(2,1)} %bitcast.25), calls=%async_computation | async-start | bytes 65536 | tf_op jit(solution)/shard_map/all_to_all | solution.py:215
  17.2 4.5 %collective-permute-start = (bf16[16,2560]{1,0:T(8,128)(2,1)S(1)}, bf16[16,2560]{1,0:T(8,128)(2,1)S(1)}, u32[]{:S(2)}, u32[]{:S(2)}) collective-permute-start(bf16[16,2560]{1,0:T(8,128)(2,1)S(1)} %convert_element_type.48), channel_id=1, source_target_pairs={{0,2},{2,0},{4,6},{6,4},{8,10},{10,8},{12,14},{14,12},{1,3},{3,1},... | collective-permute-start | bytes 245768 | tf_op jit(solution)/shard_map/ppermute | solution.py:195
  21.7 4.8 %collective-permute-start.1 = (bf16[16,2560]{1,0:T(8,128)(2,1)S(1)}, bf16[16,2560]{1,0:T(8,128)(2,1)S(1)}, u32[]{:S(2)}, u32[]{:S(2)}) collective-permute-start(bf16[16,2560]{1,0:T(8,128)(2,1)S(1)} %fusion), channel_id=1, source_target_pairs={{0,4},{2,6},{4,0},{6,2},{8,12},{10,14},{12,8},{14,10},{1,5},{3,7},... | collective-permute-start | bytes 245768 | tf_op jit(solution)/shard_map/ppermute | solution.py:195
  26.5 6.3 %collective-permute-start.2 = (bf16[16,2560]{1,0:T(8,128)(2,1)S(1)}, bf16[16,2560]{1,0:T(8,128)(2,1)S(1)}, u32[]{:S(2)}, u32[]{:S(2)}) collective-permute-start(bf16[16,2560]{1,0:T(8,128)(2,1)S(1)} %fusion.1), channel_id=1, source_target_pairs={{0,8},{2,10},{4,12},{6,14},{8,0},{10,2},{12,4},{14,6},{1,9},{3,11}... | collective-permute-start | bytes 245768 | tf_op jit(solution)/shard_map/ppermute | solution.py:195

commit v3 on v2

v3 whole, which is shorter than its diff:
```python
import functools

import jax
import jax.numpy as jnp
from jax import lax
from jax.experimental import pallas as pl
from jax.experimental.pallas import tpu as pltpu
from jax.sharding import PartitionSpec as P

HEAD_SIZE = 128
NEG_FILL = -1e30
MIB = 2**20
STAT_ROWS = 16
LOAD_LIMIT = 49 * MIB + 512 * 1024
KEEP_LIMIT = 53 * MIB

ANY = pl.BlockSpec(memory_space=pl.ANY)
VMEM = pl.BlockSpec(memory_space=pltpu.VMEM)
SMEM = pl.BlockSpec(memory_space=pltpu.SMEM)


def weight_copies(head, wq, wkv, wq_here, wkv_here, sems, pieces):
    width = wq_here.shape[1] // pieces
    first = pl.multiple_of(head * wq_here.shape[1], HEAD_SIZE)
    copies = [
        pltpu.make_async_copy(
            wq.at[:, pl.ds(first + i * width, width)],
            wq_here.at[:, pl.ds(i * width, width)],
            sems.at[i],
        )
        for i in range(pieces)
    ]
    first = pl.multiple_of(head * HEAD_SIZE, HEAD_SIZE)
    for i in range(2):
        copies.append(
            pltpu.make_async_copy(
                wkv.at[i, :, pl.ds(first, HEAD_SIZE)], wkv_here.at[i], sems.at[pieces + i]
            )
        )
    for copy in copies:
        copy.start()
    return copies


def load_kernel(pieces, head, wq, wkv, wq_here, wkv_here, sems):
    for copy in weight_copies(head[0], wq, wkv, wq_here, wkv_here, sems, pieces):
        copy.wait()


def load(head, wq, wkv, pieces):
    depth, q_width = wq.shape
    shapes = ((depth, q_width // 2), (2, depth, HEAD_SIZE))
    moved = depth * (q_width + wkv.shape[2] * 2)
    return pl.pallas_call(
        functools.partial(load_kernel, pieces),
        out_shape=[jax.ShapeDtypeStruct(shape, wq.dtype) for shape in shapes],
        in_specs=[SMEM, ANY, ANY],
        out_specs=[VMEM] * 2,
        scratch_shapes=[pltpu.SemaphoreType.DMA((pieces + 2,))],
        compiler_params=pltpu.CompilerParams(vmem_limit_bytes=LOAD_LIMIT),
        cost_estimate=pl.CostEstimate(flops=0, bytes_accessed=2 * moved, transcendentals=0),
        name="load",
    )(head, wq, wkv)


def gather_rows(rows_ref):
    if len(rows_ref.shape) == 3:
        return jnp.concatenate([rows_ref[i] for i in range(rows_ref.shape[0])], axis=0)
    return rows_ref[...]


def send_kernel(rows_ref, wq_ref, wkv_ref, out_ref):
    rows = gather_rows(rows_ref)
    first = 0
    for weights in (wq_ref, wkv_ref.at[0], wkv_ref.at[1]):
        width = weights.shape[1]
        out_ref[:, first : first + width] = jnp.dot(
            rows, weights[...], preferred_element_type=jnp.float32
        ).astype(jnp.bfloat16)
        first += width


def send_part(rows, wq_half, wkv_half):
    depth, q_width = wq_half.shape
    return pl.pallas_call(
        send_kernel,
        out_shape=jax.ShapeDtypeStruct(
            (rows.size // depth, q_width + 2 * HEAD_SIZE), jnp.bfloat16
        ),
        in_specs=[VMEM] * 3,
        out_specs=VMEM,
        compiler_params=pltpu.CompilerParams(vmem_limit_bytes=8 * MIB),
        name="send_part",
    )(rows, wq_half, wkv_half)


def keep_kernel(pieces, head, rows_ref, wq, wkv, out_ref, wq_here, wkv_here, sems):
    copies = weight_copies(head[0], wq, wkv, wq_here, wkv_here, sems, pieces)
    rows = gather_rows(rows_ref)
    q_width = wq_here.shape[1]
    width = q_width // pieces
    for i in range(pieces):
        copies[i].wait()
        out_ref[:, i * width : (i + 1) * width] = jnp.dot(
            rows, wq_here[:, i * width : (i + 1) * width], preferred_element_type=jnp.float32
        )
    for i in range(2):
        copies[pieces + i].wait()
        first = q_width + i * HEAD_SIZE
        out_ref[:, first : first + HEAD_SIZE] = jnp.dot(
            rows, wkv_here[i], preferred_element_type=jnp.float32
        )


def keep_part(head, rows, wq, wkv, pieces):
    depth, q_width = wq.shape
    half = q_width // 2
    count = rows.size // depth
    width = half + 2 * HEAD_SIZE
    return pl.pallas_call(
        functools.partial(keep_kernel, pieces),
        out_shape=jax.ShapeDtypeStruct((count, width), jnp.float32),
        in_specs=[SMEM, VMEM, ANY, ANY],
        out_specs=VMEM,
        scratch_shapes=[
            pltpu.VMEM((depth, half), wq.dtype),
            pltpu.VMEM((2, depth, HEAD_SIZE), wkv.dtype),
            pltpu.SemaphoreType.DMA((pieces + 2,)),
        ],
        compiler_params=pltpu.CompilerParams(vmem_limit_bytes=KEEP_LIMIT),
        cost_estimate=pl.CostEstimate(
            flops=2 * count * depth * width, bytes_accessed=2 * depth * width, transcendentals=0
        ),
        name="keep_part",
    )(head, rows, wq, wkv)


def attend_kernel(group, tok_dev, place, limits, query, fresh, cache, swapped, out):
    rows = fresh.shape[1]
    size = out.shape[0]
    own = query.shape[0] // size
    cache_len = cache.shape[1]
    scale = HEAD_SIZE ** (-0.5)
    here = place[0]
    head = lax.rem(here, 2)
    heads = pl.ds(pl.multiple_of(head * HEAD_SIZE, HEAD_SIZE), HEAD_SIZE)
    beside = here + 1 - 2 * head
    first_row = (here - head) * 2 * tok_dev
    q = query[...]
    contract = (((1,), (1,)), ((), ()))
    slot = lax.broadcasted_iota(jnp.int32, (query.shape[0], cache_len), 1)

    def scored(keys, first_slot):
        scores = scale * lax.dot_general(q, keys, contract, preferred_element_type=jnp.float32)
        return jnp.where(slot < limits[0] - first_slot, scores, NEG_FILL)

    near_shape = (query.shape[0], rows)
    row = lax.broadcasted_iota(jnp.int32, near_shape, 0) // group
    key = lax.broadcasted_iota(jnp.int32, near_shape, 1)
    filled = jnp.where(key % 2 == 0, limits[1], limits[2])
    seen = (
        (row >= first_row)
        & (row < first_row + 4 * tok_dev)
        & (key % 2 == row % 2)
        & (key // 2 <= row // 2)
        & (key // 2 < filled)
    )
    near = scale * lax.dot_general(q, fresh[0], contract, preferred_element_type=jnp.float32)
    parts = (
        (scored(cache[0, :, heads], here * cache_len), cache[1, :, heads]),
        (scored(swapped[0], beside * cache_len), swapped[1]),
        (jnp.where(seen, near, NEG_FILL), fresh[1]),
    )
    peak = functools.reduce(
        jnp.maximum, (jnp.max(scores, axis=1, keepdims=True) for scores, _ in parts)
    )
    base = jnp.maximum(peak, NEG_FILL / 10)
    total = jnp.zeros_like(peak)
    acc = jnp.zeros((query.shape[0], HEAD_SIZE), jnp.float32)
    for scores, values in parts:
        weights = jnp.exp(scores - base)
        total = total + jnp.sum(weights, axis=1, keepdims=True)
        acc = acc + jnp.dot(
            weights.astype(jnp.bfloat16), values, preferred_element_type=jnp.float32
        )
    some = total > 0.0
    safe = jnp.where(some, total, 1.0)
    lse = jnp.where(some, base + jnp.log(safe), NEG_FILL)
    out[:, :own, :] = (acc / safe).astype(jnp.bfloat16).reshape(size, own, HEAD_SIZE)
    lane = lax.broadcasted_iota(jnp.int32, (own, HEAD_SIZE), 1)
    line = lax.broadcasted_iota(jnp.int32, (own, HEAD_SIZE), 0)
    spread = jnp.broadcast_to(lse, (size * own, HEAD_SIZE)).reshape(size, own, HEAD_SIZE)
    stats = jnp.sum(jnp.where((lane == line)[None], spread, 0.0), axis=1)
    high = stats.astype(jnp.bfloat16).astype(jnp.float32)
    rest = stats - high
    middle = rest.astype(jnp.bfloat16).astype(jnp.float32)
    low = rest - middle
    which = lax.broadcasted_iota(jnp.int32, (size, STAT_ROWS, HEAD_SIZE), 1)
    terms = jnp.where(
        which == 0, high[:, None, :], jnp.where(which == 1, middle[:, None, :], low[:, None, :])
    )
    out[:, own:, :] = terms.astype(jnp.bfloat16)


def attend(place, limits, query, fresh, cache, swapped, size, group, tok_dev):
    own = query.shape[0] // size
    return pl.pallas_call(
        functools.partial(attend_kernel, group, tok_dev),
        out_shape=jax.ShapeDtypeStruct((size, own + STAT_ROWS, HEAD_SIZE), jnp.bfloat16),
        in_specs=[SMEM, SMEM, VMEM, VMEM, VMEM, VMEM],
        out_specs=VMEM,
        compiler_params=pltpu.CompilerParams(
            vmem_limit_bytes=8 * MIB if query.shape[0] <= 256 else 48 * MIB
        ),
        name="attend",
    )(place, limits, query, fresh, cache, swapped)


def combine_kernel(group, tok_dev, place, limits, parts, out):
    size = parts.shape[0]
    own = out.shape[1]
    stats = (
        parts[:, own, :].astype(jnp.float32)
        + parts[:, own + 1, :].astype(jnp.float32)
        + parts[:, own + 2, :].astype(jnp.float32)
    )
    odd = lax.broadcasted_iota(jnp.int32, stats.shape, 0) % 2 == 1
    peaks = [
        jnp.max(jnp.where(odd == bool(g), stats, 2 * NEG_FILL), axis=0, keepdims=True)
        for g in range(2)
    ]
    weights = jnp.exp(stats - jnp.where(odd, peaks[1], peaks[0]))
    totals = [
        jnp.sum(jnp.where(odd == bool(g), weights, 0.0), axis=0, keepdims=True) for g in range(2)
    ]
    weights = weights / jnp.where(odd, totals[1], totals[0])
    row = (lax.broadcasted_iota(jnp.int32, stats.shape, 1) % own) // group
    filled = jnp.where(row % 2 == 0, limits[1], limits[2])
    weights = jnp.where(place[0] * tok_dev + row // 2 < filled, weights, 0.0)
    mask = lax.broadcasted_iota(jnp.int32, (own, HEAD_SIZE), 0) == lax.broadcasted_iota(
        jnp.int32, (own, HEAD_SIZE), 1
    )
    column = jnp.sum(jnp.where(mask[None], weights[:, None, :], 0.0), axis=2, keepdims=True)
    scaled = column * parts[:, :own, :].astype(jnp.float32)
    out[...] = jnp.sum(scaled.reshape(size // 2, 2, own, HEAD_SIZE), axis=0)


def combine(place, limits, parts, group, tok_dev):
    own = parts.shape[1] - STAT_ROWS
    return pl.pallas_call(
        functools.partial(combine_kernel, group, tok_dev),
        out_shape=jax.ShapeDtypeStruct((2, own, HEAD_SIZE), jnp.float32),
        in_specs=[SMEM, SMEM, VMEM],
        out_specs=VMEM,
        compiler_params=pltpu.CompilerParams(vmem_limit_bytes=8 * MIB),
        name="combine",
    )(place, limits, parts)


def swap(value, axis, size, bit):
    return lax.ppermute(value, axis, [(d, d ^ bit) for d in range(size)])


def shards(hidden, wq, wkv, bias_q, bias_kv, key_value_cache, prompt_len, resp_len):
    tok_dev = hidden.shape[0]
    size = lax.axis_size("ctx")
    here = lax.axis_index("ctx").astype(jnp.int32)
    q_width = wq.shape[1]
    k_width = wkv.shape[2]
    group = q_width // k_width
    half = q_width // 2
    row_count = 2 * tok_dev
    rows = row_count * size
    if k_width != 2 * HEAD_SIZE or size & (size - 1) or size < 2:
        raise ValueError("unsupported shapes")
    place = here.reshape(1)
    head = here % 2
    limits = jnp.concatenate((prompt_len, resp_len))

    sent = hidden.reshape(row_count, size, hidden.shape[2] // size)
    columns = lax.all_to_all(sent, "ctx", split_axis=1, concat_axis=1, tiled=True)
    columns = jnp.swapaxes(columns, 0, 1)
    if size > 16:
        columns = columns.reshape(rows, columns.shape[2])

    other = (1 - head) * HEAD_SIZE
    swapped = swap(
        lax.dynamic_slice_in_dim(key_value_cache, other, HEAD_SIZE, 2), "ctx", size, 1
    )
    wq_half, wkv_half = load((1 - head).reshape(1), wq, wkv, 2)
    received = swap(send_part(columns, wq_half, wkv_half), "ctx", size, 1)
    kept = keep_part(head.reshape(1), columns, wq, wkv, 4)
    value = kept + received.astype(jnp.float32)
    bit = 2
    while bit < size:
        received = swap(value.astype(jnp.bfloat16), "ctx", size, bit)
        value = value + received.astype(jnp.float32)
        bit *= 2
    bias = jnp.concatenate(
        (
            lax.dynamic_slice_in_dim(bias_q, head * half, half),
            lax.dynamic_slice_in_dim(bias_kv, head * HEAD_SIZE, HEAD_SIZE, 1).reshape(-1),
        )
    ).astype(jnp.float32)
    projected = (value + bias).astype(jnp.bfloat16)
    query = projected[:, :half].reshape(rows * group, HEAD_SIZE)
    fresh = jnp.stack((projected[:, half : half + HEAD_SIZE], projected[:, half + HEAD_SIZE :]))
    parts = attend(place, limits, query, fresh, key_value_cache, swapped, size, group, tok_dev)
    parts = lax.all_to_all(parts, "ctx", split_axis=0, concat_axis=0, tiled=True)
    result = combine(place, limits, parts, group, tok_dev)
    result = result.reshape(2, row_count, group, HEAD_SIZE)
    result = jnp.transpose(result, (1, 0, 2, 3))
    return result.reshape(tok_dev, 2, q_width).astype(jnp.bfloat16)


def solution(mesh):
    return jax.shard_map(
        shards,
        mesh=mesh,
        in_specs=(
            P(("pairs", "ctx"), None, None),
            P("ctx", "head"),
            P(None, "ctx", "head"),
            P("head"),
            P(None, "head"),
            P(None, ("pairs", "ctx"), "head"),
            P("pairs"),
            P("pairs"),
        ),
        out_specs=P(("pairs", "ctx"), None, "head"),
        check_vma=False,
    )
```

time: 45.4 us -> 42.7 us (0.941)
  waiting for transfers between devices: 19.8 us -> 6.25 us
  starting transfers between devices: 9.15 us -> 13.4 us
  local copies, waits for them, and re-layouts: 0.68 us -> 3.54 us
  blocking collectives: 9.51 us -> 12.1 us
  Pallas kernels: 5.02 us -> 6.21 us
    ppermute x3 -> x4, waiting for transfers between devices: 13.8 us -> 5.97 us  [swap(): return lax.ppermute(value, axis, [(d, d ^ bit) for d in range(size)])]
    all_to_all x1, waiting for transfers between devices: 6.03 us -> 0.28 us  [shards(): lax.all_to_all(sent, 'ctx', split_axis=1, concat_axis=1, tiled=True)]
    ppermute x3 -> x4, starting transfers between devices: 1.71 us -> 5.97 us  [swap(): return lax.ppermute(value, axis, [(d, d ^ bit) for d in range(size)])]
    all_to_all x1, blocking collectives: 9.51 us -> 12.1 us  [shards(): lax.all_to_all(parts, 'ctx', split_axis=0, concat_axis=0, tiled=True)]
    dynamic_slice x0 -> x3, local copies, waits for them, and re-layouts: none -> 1.67 us  [the longest x1 1.66 us: shards(): lax.dynamic_slice_in_dim(key_value_cache, other, HEAD_SIZE, 2)]
    unnamed x10 -> x8, local copies, waits for them, and re-layouts: 0.03 us -> 1.24 us
    pallas_call x3 -> x5, Pallas kernels: 5.02 us -> 6.21 us  [the longest x1 2.43 us: keep_part(): pl.pallas_call(functools.partial(keep_kernel, pieces), out_shape=jax.Shap...]
  transfers between devices with their start and end apart: 4 -> 5, of which waited for: 4 -> 4; matrix products, arithmetic and copies ran while one was open for 0% -> 4% of each run, Pallas kernels for 0% -> 11%
where the time goes in v3:
time: 42.7 us; the launch traced here: 42.4 us
  starting transfers between devices  13.4 us (31%)
  blocking collectives  12.1 us (28%)
  waiting for transfers between devices  6.25 us (15%)
  Pallas kernels  6.21 us (15%)
  local copies, waits for them, and re-layouts  3.54 us (8%)
  between operations  0.77 us (2%)
    all_to_all x1, blocking collectives, shards(): lax.all_to_all(parts, 'ctx', split_axis=0, concat_axis=0, tiled=True)  12.1 us
    all_to_all x1, starting transfers between devices, shards(): lax.all_to_all(sent, 'ctx', split_axis=1, concat_axis=1, tiled=True)  7.41 us
    ppermute x4, waiting for transfers between devices, swap(): return lax.ppermute(value, axis, [(d, d ^ bit) for d in range(size)])  5.97 us
    ppermute x4, starting transfers between devices, swap(): return lax.ppermute(value, axis, [(d, d ^ bit) for d in range(size)])  5.97 us
    pallas_call x1, Pallas kernels, keep_part(): pl.pallas_call(functools.partial(keep_kernel, pieces), out_shape=jax.Shap...  2.43 us
    dynamic_slice x1, local copies, waits for them, and re-layouts, shards(): lax.dynamic_slice_in_dim(key_value_cache, other, HEAD_SIZE, 2)  1.66 us
    pallas_call x1, Pallas kernels, load(): pl.pallas_call(functools.partial(load_kernel, pieces), out_shape=[jax.Sha...  1.59 us
    unnamed x8, local copies, waits for them, and re-layouts  1.24 us
  transfers between devices with their start and end apart: 5, of which 4 were waited for; matrix products, arithmetic and copies ran while one was open for 4% of the time, Pallas kernels for 11%

profile of v3, /device:TPU:0, one launch (start us, length us, event | category | flops | bytes accessed | tf_op | source)
XLA Modules:
  0.0 42.4 jit_solution(3826322560845819576)
XLA Ops:
  0.0 0.0 copy-start
  0.0 7.4 %all-to-all-start = ((bf16[2,8,1024]{2,0,1:T(2,128)(2,1)}), bf16[2,8,1024]{2,0,1:T(2,128)(2,1)S(1)}, u32[]{:S(2)}, u32[]{:S(2)}) async-start(bf16[2,8,1024]{2,0,1:T(2,128)(2,1)} %bitcast.19), calls=%async_computation | async-start | bytes 65536 | tf_op jit(solution)/shard_map/all_to_all | solution.py:281
  7.4 1.7 %constant_dynamic-slice_fusion = bf16[2,512,128]{2,1,0:T(8,128)(2,1)} fusion(bf16[2,512,256]{2,1,0:T(8,128)(2,1)} %cache.1, s32[]{:T(128)S(6)} %select_n.19), kind=kLoop, calls=%fused_computation.12 | loop fusion | bytes 524292 | tf_op jit(solution)/shard_map/dynamic_slice | solution.py:288
  9.1 2.0 %collective-permute-start.3 = (bf16[2,512,128]{2,1,0:T(8,128)(2,1)}, bf16[2,512,128]{2,1,0:T(8,128)(2,1)S(1)}, u32[]{:S(2)}, u32[]{:S(2)}) collective-permute-start(bf16[2,512,128]{2,1,0:T(8,128)(2,1)} %constant_dynamic-slice_fusion), channel_id=1, source_target_pairs={{0,2},{2,0},{4,6},{6,4},{8,10},{10,8},{12,14},{14,12},{1,3},{3,1},... | collective-permute-start | bytes 786440 | tf_op jit(solution)/shard_map/ppermute | solution.py:261
  11.1 0.0 copy-start.1
  11.1 1.2 %copy-done.1 = bf16[2,1024,256]{2,1,0:T(8,128)(2,1)S(1)} copy-done((bf16[2,1024,256]{2,1,0:T(8,128)(2,1)S(1)}, bf16[2,1024,256]{2,1,0:T(8,128)(2,1)}, u32[]{:S(2)}) %copy-start.1) | copy-done | bytes 1048600
  12.3 1.6 %load.1 = (bf16[1024,1024]{1,0:T(8,128)(2,1)S(1)}, bf16[2,1024,128]{2,1,0:T(8,128)(2,1)S(1)}) custom-call(s32[1]{0:T(128)} %bitcast.4.head, bf16[1024,2048]{1,0:T(8,128)(2,1)} %wq.3, bf16[2,1024,256]{2,1,0:T(8,128)(2,1)S(1)} %copy-done.1), custom_call_target="tpu_custom_call" | custom-call | bytes 5242880 | tf_op jit(solution)/shard_map/load/pallas_call | solution.py:54
  13.9 0.3 all-to-all-done
  14.2 0.0 copy-start.3
  14.2 0.0 copy-start.2
  14.2 0.4 %send_part.1 = bf16[16,1280]{1,0:T(8,128)(2,1)S(1)} custom-call(bf16[8,2,1024]{2,1,0:T(2,128)(2,1)S(1)} %bitcast.17, bf16[1024,1024]{1,0:T(8,128)(2,1)S(1)} %get-tuple-element.7.wq_ref, bf16[2,1024,128]{2,1,0:T(8,128)(2,1)S(1)} %get-tuple-element.8.wkv_ref), custom_call_target="tpu_custom_call" | custom-call | tf_op jit(solution)/shard_map/send_part/pallas_call | solution.py:85
  14.6 0.5 %collective-permute-start = (bf16[16,1280]{1,0:T(8,128)(2,1)S(1)}, bf16[16,1280]{1,0:T(8,128)(2,1)S(1)}, u32[]{:S(2)}, u32[]{:S(2)}) collective-permute-start(bf16[16,1280]{1,0:T(8,128)(2,1)S(1)} %send_part.1), channel_id=1, source_target_pairs={{0,2},{2,0},{4,6},{6,4},{8,10},{10,8},{12,14},{14,12},{1,3},{3,1},... | collective-permute-start | bytes 122888 | tf_op jit(solution)/shard_map/ppermute | solution.py:261
  15.1 0.0 copy-done
  15.1 0.0 dynamic-slice-start
  15.1 2.4 %keep_part.1 = f32[16,1280]{1,0:T(8,128)S(1)} custom-call(s32[1]{0:T(128)} %bitcast.1.head, bf16[8,2,1024]{2,1,0:T(2,128)(2,1)S(1)} %bitcast.18, bf16[1024,2048]{1,0:T(8,128)(2,1)} %wq.3, bf16[2,1024,256]{2,1,0:T(8,128)(2,1)} %wkv.3), custom_call_target="tpu_custom_call" | custom-call | flops 41943040 | bytes 2621440 | tf_op jit(solution)/shard_map/keep_part/pallas_call | solution.py:120
  17.6 1.1 %collective-permute-done = bf16[16,1280]{1,0:T(8,128)(2,1)S(1)} collective-permute-done((bf16[16,1280]{1,0:T(8,128)(2,1)S(1)}, bf16[16,1280]{1,0:T(8,128)(2,1)S(1)}, u32[]{:S(2)}, u32[]{:S(2)}) %collective-permute-start) | collective-permute-done | bytes 40992 | tf_op jit(solution)/shard_map/ppermute | solution.py:261
  18.7 1.3 %collective-permute-start.1 = (bf16[16,1280]{1,0:T(8,128)(2,1)S(1)}, bf16[16,1280]{1,0:T(8,128)(2,1)S(1)}, u32[]{:S(2)}, u32[]{:S(2)}) collective-permute-start(bf16[16,1280]{1,0:T(8,128)(2,1)S(1)} %fusion), channel_id=1, source_target_pairs={{0,4},{2,6},{4,0},{6,2},{8,12},{10,14},{12,8},{14,10},{1,5},{3,7},... | collective-permute-start | bytes 122888 | tf_op jit(solution)/shard_map/ppermute | solution.py:261
  20.0 0.0 dynamic-slice-done
  20.7 2.1 %collective-permute-done.1 = bf16[16,1280]{1,0:T(8,128)(2,1)S(1)} collective-permute-done((bf16[16,1280]{1,0:T(8,128)(2,1)S(1)}, bf16[16,1280]{1,0:T(8,128)(2,1)S(1)}, u32[]{:S(2)}, u32[]{:S(2)}) %collective-permute-start.1) | collective-permute-done | bytes 40992 | tf_op jit(solution)/shard_map/ppermute | solution.py:261
  22.8 2.2 %collective-permute-start.2 = (bf16[16,1280]{1,0:T(8,128)(2,1)S(1)}, bf16[16,1280]{1,0:T(8,128)(2,1)S(1)}, u32[]{:S(2)}, u32[]{:S(2)}) collective-permute-start(bf16[16,1280]{1,0:T(8,128)(2,1)S(1)} %fusion.1), channel_id=1, source_target_pairs={{0,8},{2,10},{4,12},{6,14},{8,0},{10,2},{12,4},{14,6},{1,9},{3,11}... | collective-permute-start | bytes 122888 | tf_op jit(solution)/shard_map/ppermute | solution.py:261
  25.0 0.0 copy-done.3
  25.0 0.1 pad_add_fusion.limits
  25.1 2.7 %collective-permute-done.2 = bf16[16,1280]{1,0:T(8,128)(2,1)S(1)} collective-permute-done((bf16[16,1280]{1,0:T(8,128)(2,1)S(1)}, bf16[16,1280]{1,0:T(8,128)(2,1)S(1)}, u32[]{:S(2)}, u32[]{:S(2)}) %collective-permute-start.2) | collective-permute-done | bytes 40992 | tf_op jit(solution)/shard_map/ppermute | solution.py:261
  27.9 0.0 collective-permute-done.3.swapped
  27.9 0.0 copy-done.2
  27.9 1.1 %attend.1 = bf16[8,32,128]{2,1,0:T(8,128)(2,1)S(1)} custom-call(s32[1]{0:T(128)} %bitcast.place, s32[3]{0:T(128)S(1)} %pad_add_fusion.limits, bf16[128,128]{1,0:T(8,128)(2,1)S(1)} %reshape.52.query, bf16[2,16,128]{2,1,0:T(8,128)(2,1)S(1)} %pad_maximum_fusion.fresh, bf16[2,512,256]{2,1,0:T(8,128)(2,1)S(1)} %copy-done.2, ...), custom_call_target="tpu_custom_call" | custom-call | tf_op jit(solution)/shard_map/attend/pallas_call | solution.py:207
  29.0 12.1 %all_to_all.10.parts = bf16[8,32,128]{2,1,0:T(8,128)(2,1)S(1)} all-to-all(bf16[8,32,128]{2,1,0:T(8,128)(2,1)S(1)} %attend.1), channel_id=1, replica_groups=mesh['pairs'=2,'ctx'=8,'head'=2] {'ctx'}, dimensions={0} | all-to-all | bytes 131072 | tf_op jit(solution)/shard_map/all_to_all | solution.py:309
  41.1 0.7 %combine.1 = f32[2,16,128]{2,1,0:T(8,128)S(1)} custom-call(s32[1]{0:T(128)} %bitcast.place, s32[3]{0:T(128)S(1)} %pad_add_fusion.limits, bf16[8,32,128]{2,1,0:T(8,128)(2,1)S(1)} %all_to_all.10.parts), custom_call_target="tpu_custom_call" | custom-call | tf_op jit(solution)/shard_map/combine/pallas_call | solution.py:250
  41.8 0.6 %convert_element_type.55 = bf16[1,2,2048]{2,1,0:T(2,128)(2,1)} reshape(bf16[2,2,8,128]{3,2,1,0:T(8,128)(2,1)S(1)} %copy.9) | data formatting | bytes 16384 | tf_op jit(solution)/shard_map/convert_element_type | solution.py:313
  (11 shorter events, 0.1 us)
Async XLA Ops:
  0.0 15.1 %copy-start = (bf16[2,256]{1,0:T(2,128)(2,1)S(1)}, bf16[2,256]{1,0:T(2,128)(2,1)}, u32[]{:S(2)}) copy-start(bf16[2,256]{1,0:T(2,128)(2,1)} %param.12) | copy-start | bytes 3076
  0.0 14.2 %all-to-all-start = ((bf16[2,8,1024]{2,0,1:T(2,128)(2,1)}), bf16[2,8,1024]{2,0,1:T(2,128)(2,1)S(1)}, u32[]{:S(2)}, u32[]{:S(2)}) async-start(bf16[2,8,1024]{2,0,1:T(2,128)(2,1)} %bitcast.19), calls=%async_computation | async-start | bytes 65536 | tf_op jit(solution)/shard_map/all_to_all | solution.py:281
  9.1 18.8 %collective-permute-start.3 = (bf16[2,512,128]{2,1,0:T(8,128)(2,1)}, bf16[2,512,128]{2,1,0:T(8,128)(2,1)S(1)}, u32[]{:S(2)}, u32[]{:S(2)}) collective-permute-start(bf16[2,512,128]{2,1,0:T(8,128)(2,1)} %constant_dynamic-slice_fusion), channel_id=1, source_target_pairs={{0,2},{2,0},{4,6},{6,4},{8,10},{10,8},{12,14},{14,12},{1,3},{3,1},... | collective-permute-start | bytes 786440 | tf_op jit(solution)/shard_map/ppermute | solution.py:261
  11.1 1.2 %copy-start.1 = (bf16[2,1024,256]{2,1,0:T(8,128)(2,1)S(1)}, bf16[2,1024,256]{2,1,0:T(8,128)(2,1)}, u32[]{:S(2)}) copy-start(bf16[2,1024,256]{2,1,0:T(8,128)(2,1)} %wkv.3) | copy-start | bytes 3145732
  14.2 10.8 %copy-start.3 = (s32[2]{0:T(128)S(1)}, s32[2]{0:T(128)}, u32[]{:S(2)}) copy-start(s32[2]{0:T(128)} %param.15) | copy-start | bytes 28
  14.2 13.7 %copy-start.2 = (bf16[2,512,256]{2,1,0:T(8,128)(2,1)S(1)}, bf16[2,512,256]{2,1,0:T(8,128)(2,1)}, u32[]{:S(2)}) copy-start(bf16[2,512,256]{2,1,0:T(8,128)(2,1)} %cache.1) | copy-start | bytes 1572868
  14.6 4.1 %collective-permute-start = (bf16[16,1280]{1,0:T(8,128)(2,1)S(1)}, bf16[16,1280]{1,0:T(8,128)(2,1)S(1)}, u32[]{:S(2)}, u32[]{:S(2)}) collective-permute-start(bf16[16,1280]{1,0:T(8,128)(2,1)S(1)} %send_part.1), channel_id=1, source_target_pairs={{0,2},{2,0},{4,6},{6,4},{8,10},{10,8},{12,14},{14,12},{1,3},{3,1},... | collective-permute-start | bytes 122888 | tf_op jit(solution)/shard_map/ppermute | solution.py:261
  15.1 4.9 %dynamic-slice-start = ((bf16[2048]{0:T(1024)(128)(2,1)}, s32[]{:T(128)}), bf16[1024]{0:T(1024)(128)(2,1)S(1)}, s32[]{:S(2)}) async-start(bf16[2048]{0:T(1024)(128)(2,1)} %param.11, s32[]{:T(128)} %select_n.17), calls=%async_computation.2 | async-start | bytes 4608 | tf_op jit(solution)/shard_map/dynamic_slice | solution.py:301
  18.7 4.1 %collective-permute-start.1 = (bf16[16,1280]{1,0:T(8,128)(2,1)S(1)}, bf16[16,1280]{1,0:T(8,128)(2,1)S(1)}, u32[]{:S(2)}, u32[]{:S(2)}) collective-permute-start(bf16[16,1280]{1,0:T(8,128)(2,1)S(1)} %fusion), channel_id=1, source_target_pairs={{0,4},{2,6},{4,0},{6,2},{8,12},{10,14},{12,8},{14,10},{1,5},{3,7},... | collective-permute-start | bytes 122888 | tf_op jit(solution)/shard_map/ppermute | solution.py:261
  22.8 5.0 %collective-permute-start.2 = (bf16[16,1280]{1,0:T(8,128)(2,1)S(1)}, bf16[16,1280]{1,0:T(8,128)(2,1)S(1)}, u32[]{:S(2)}, u32[]{:S(2)}) collective-permute-start(bf16[16,1280]{1,0:T(8,128)(2,1)S(1)} %fusion.1), channel_id=1, source_target_pairs={{0,8},{2,10},{4,12},{6,14},{8,0},{10,2},{12,4},{14,6},{1,9},{3,11}... | collective-permute-start | bytes 122888 | tf_op jit(solution)/shard_map/ppermute | solution.py:261
